TPU v7x, 32 devices: a whole 2x2x4 slice. The times are simulated.
32 devices in a mesh: dp: 4 (over x, core), expert: 8 (over z, y).
Axes of the slice: x: 2, y: 2, z: 4, core: 2. Of those that a mesh axis runs over, the one named last changes fastest.
Arguments:
- tokens: bfloat16 [6144, 1024], P(('dp', 'expert')), may hold values from -6 to 6
- route_ids: int32 [6144, 4], P(('dp', 'expert')), may hold values from 0 to 7, all different within a row; in each aligned block of 192 rows (0 to 191, 192 to 383, ...) at most 144 rows name the same one
- gate_weight: float32 [6144, 4], P(('dp', 'expert')), may hold values from 0.25 to 1
- old_owner: int32 [8], replicated, may hold values from 0 to 7, as said below
- new_owner: int32 [8], replicated, may hold values from 0 to 7, as said below
- weights: bfloat16 [8, 3, 1024, 1024], P('expert', None, None, 'dp'), may hold values from -0.1875 to 0.1875
- first_moment: float32 [8, 3, 1024, 1024], P('expert', None, None, 'dp'), may hold values from -6 to 6
- second_moment: float32 [8, 3, 1024, 1024], P('expert', None, None, 'dp'), may hold values from 0.01 to 4
Outputs:
- layer_output: bfloat16 [6144, 1024], P(('dp', 'expert'))
- new_weights: bfloat16 [8, 3, 1024, 1024], P('expert', None, None, 'dp')
- new_first_moment: float32 [8, 3, 1024, 1024], P('expert', None, None, 'dp')
- new_second_moment: float32 [8, 3, 1024, 1024], P('expert', None, None, 'dp')
Inputs may be any that keep to these rules, and one draw needn't show every extreme that they name: `old_owner`: A permutation of the slots. `new_owner`: A permutation of the slots that differs from old_owner in exactly 2 experts. `route_ids`: the 4 experts of a row differ. In the 192 rows of one device no expert is named more than 144 times, a bound that some block reaches.
All inputs are finite; a program needn't handle non-finite values.
Results may differ from a plain program's by a relative error of at most 0.0058.
Values may be sent and summed in bfloat16 or wider, within the bound.
No kernel may reach another device: no remote copies, remote signals or barrier semaphores. Data moves between devices by JAX's collectives and lax.ppermute only.
A program may use at most 128 MiB of HBM per device.

v0:
```python
import jax
import jax.numpy as jnp
from jax import lax
from jax.sharding import PartitionSpec as P


def relocate_weights(weights, source_slot):
    spread = lax.all_to_all(weights, "expert", split_axis=2, concat_axis=0, tiled=True)
    ordered = jnp.take(spread, source_slot, axis=0)
    return lax.all_to_all(ordered, "expert", split_axis=0, concat_axis=2, tiled=True)


def relocate_moments(first_moment, second_moment, source_slot):
    spread = (
        lax.all_to_all(first_moment, "expert", split_axis=2, concat_axis=0, tiled=True),
        lax.all_to_all(second_moment, "expert", split_axis=2, concat_axis=0, tiled=True),
    )
    ordered = (jnp.take(spread[0], source_slot, axis=0), jnp.take(spread[1], source_slot, axis=0))
    back = (
        lax.all_to_all(ordered[0], "expert", split_axis=0, concat_axis=2, tiled=True),
        lax.all_to_all(ordered[1], "expert", split_axis=0, concat_axis=2, tiled=True),
    )
    return (back[0], back[1])


def per_device(
    tokens, route_ids, gate_weight, old_owner, new_owner, weights, first_moment, second_moment
):
    peer_count = lax.axis_size("expert")
    tok_rows = tokens.shape[0]
    top_count = route_ids.shape[1]
    experts = old_owner.shape[0]
    capacity = max(2, 3 * tok_rows * top_count // (2 * experts))
    labels = jnp.arange(experts, dtype=jnp.int32)
    source_slot = jnp.sum(
        jnp.where(new_owner[None, :] == labels[:, None], old_owner[None, :], 0), axis=1
    )
    moved_first, moved_second = relocate_moments(first_moment, second_moment, source_slot)
    moved_weights = relocate_weights(weights, source_slot)
    expert_ids = route_ids.reshape(-1)
    target = jnp.sum(
        jnp.where(expert_ids[:, None] == labels[None, :], old_owner[None, :], 0), axis=1
    )
    matches = (target[:, None] == labels[None, :]).astype(jnp.int32)
    position = jnp.sum((jnp.cumsum(matches, axis=0) - 1) * matches, axis=1)
    slot_index = target * capacity + position
    slot_grid = slot_index.reshape(tok_rows, top_count)
    buffer_slots = jnp.arange(peer_count * capacity, dtype=jnp.int32)
    placement = jnp.any(slot_grid[None, :, :] == buffer_slots[:, None, None], axis=2).astype(
        jnp.bfloat16
    )
    outgoing = jnp.dot(placement, tokens, preferred_element_type=jnp.float32).astype(jnp.bfloat16)
    outgoing = outgoing.reshape(peer_count, capacity, tokens.shape[1])
    incoming = lax.all_to_all(outgoing, "expert", split_axis=0, concat_axis=0, tiled=True)
    received_rows = incoming.reshape(peer_count * capacity, tokens.shape[1])
    shard_piece = lax.all_gather(weights, "dp", axis=3, tiled=True)
    gate_part = jnp.dot(received_rows, shard_piece[0, 0], preferred_element_type=jnp.float32)
    up_part = jnp.dot(received_rows, shard_piece[0, 1], preferred_element_type=jnp.float32)
    hidden = (jax.nn.silu(gate_part) * up_part).astype(jnp.bfloat16)
    accumulated = jnp.einsum(
        "rh,dh->rd", hidden, shard_piece[0, 2], preferred_element_type=jnp.float32
    )
    answers = accumulated.astype(jnp.bfloat16).reshape(peer_count, capacity, tokens.shape[1])
    returned = lax.all_to_all(answers, "expert", split_axis=0, concat_axis=0, tiled=True)
    returned = returned.reshape(peer_count * capacity, tokens.shape[1])
    picked = (
        jnp.take(returned, slot_index, axis=0)
        .astype(jnp.float32)
        .reshape(tok_rows, top_count, tokens.shape[1])
    )
    layer_output = jnp.sum(picked * gate_weight[:, :, None], axis=1).astype(jnp.bfloat16)
    return (layer_output, moved_weights, moved_first, moved_second)


def solution(mesh):
    placed = (
        P(("dp", "expert"), None),
        P(("dp", "expert"), None),
        P(("dp", "expert"), None),
        P(),
        P(),
        P("expert", None, None, "dp"),
        P("expert", None, None, "dp"),
        P("expert", None, None, "dp"),
    )
    return jax.shard_map(
        per_device,
        mesh=mesh,
        in_specs=placed,
        out_specs=(
            P(("dp", "expert"), None),
            P("expert", None, None, "dp"),
            P("expert", None, None, "dp"),
            P("expert", None, None, "dp"),
        ),
        check_vma=False,
    )
```

profile of v0, /device:TPU:1, one launch (start us, length us, event | category | flops | bytes accessed | tf_op | source)
XLA Modules:
  0.0 582.8 jit_solution(2629963094844566343)
XLA Ops:
  7.2 0.0 copy-start
  7.2 0.0 copy-start.7
  7.2 0.0 copy-start.9
  7.2 4.1 copy.50
  11.3 6.4 %all-to-all-start.2 = ((bf16[1,3,1024,256]{3,1,0,2:T(4,128)(2,1)}), bf16[1,3,1024,256]{3,1,0,2:T(4,128)(2,1)S(1)}, u32[]{:S(2)}, u32[]{:S(2)}) async-start(bf16[1,3,1024,256]{3,1,0,2:T(4,128)(2,1)} %copy.50), calls=%async_computation.2 | async-start | bytes 4194304 | tf_op jit(solution)/shard_map/all_to_all | solution.py:8
  17.7 0.0 copy-done.7
  17.7 0.1 copy.45
  17.8 0.1 eq.64
  17.9 0.0 copy-done.9
  18.0 0.1 select_reduce_fusion
  18.0 1.7 reduce-window.6
  19.8 0.1 slice.28
  19.8 0.1 copy.46
  20.0 0.2 reduce-window.9
  20.1 0.1 copy.47
  20.2 0.1 fusion.3
  20.3 0.1 add.71
  20.4 0.0 copy-start.5
  20.5 0.1 copy.48
  20.5 0.6 fusion.1
  21.2 0.0 copy-done
  21.2 2.2 convolution_convert_fusion.1
  23.4 41.7 %all-to-all-done.2 = bf16[1,3,1024,256]{3,1,0,2:T(4,128)(2,1)S(1)} async-done(((bf16[1,3,1024,256]{3,1,0,2:T(4,128)(2,1)}), bf16[1,3,1024,256]{3,1,0,2:T(4,128)(2,1)S(1)}, u32[]{:S(2)}, u32[]{:S(2)}) %all-to-all-start.2) | async-done | bytes 1572896 | tf_op jit(solution)/shard_map/all_to_all | solution.py:8
  65.1 0.0 copy-done.5
  65.1 4.6 all-to-all-start
  69.8 6.0 %copy.54 = f32[1,3,1024,256]{3,1,0,2:T(4,128)} copy(f32[1,3,1024,256]{3,2,1,0:T(8,128)} %param.16) | data formatting | bytes 6291456 | tf_op args[6]
  75.8 46.7 %all-to-all-done = bf16[8,144,1024]{2,1,0:T(8,128)(2,1)} async-done(((bf16[8,144,1024]{2,1,0:T(8,128)(2,1)}), bf16[8,144,1024]{2,1,0:T(8,128)(2,1)}, u32[]{:S(2)}, u32[]{:S(2)}) %all-to-all-start) | async-done | bytes 2359328 | tf_op jit(solution)/shard_map/all_to_all | solution.py:54
  122.5 5.1 all-to-all-start.4
  127.5 6.1 %copy.58 = f32[1,3,1024,256]{3,1,0,2:T(4,128)} copy(f32[1,3,1024,256]{3,2,1,0:T(8,128)} %param.17) | data formatting | bytes 6291456 | tf_op args[7]
  133.6 85.7 %all-to-all-done.4 = f32[1,3,1024,256]{3,1,0,2:T(4,128)} async-done(((f32[1,3,1024,256]{3,1,0,2:T(4,128)}), f32[1,3,1024,256]{3,1,0,2:T(4,128)}, u32[]{:S(2)}, u32[]{:S(2)}) %all-to-all-start.4) | async-done | bytes 3145760 | tf_op jit(solution)/shard_map/all_to_all | solution.py:15
  219.4 5.3 all-to-all-start.6
  224.6 0.0 copy-done.10
  224.7 0.1 select_reduce_fusion.1
  224.8 1.5 copy.73
  226.2 2.1 gather_fusion.1
  228.3 1.4 broadcast_select_fusion.2
  229.7 86.8 %all-to-all-done.6 = f32[1,3,1024,256]{3,1,0,2:T(4,128)} async-done(((f32[1,3,1024,256]{3,1,0,2:T(4,128)}), f32[1,3,1024,256]{3,1,0,2:T(4,128)}, u32[]{:S(2)}, u32[]{:S(2)}) %all-to-all-start.6) | async-done | bytes 3145760 | tf_op jit(solution)/shard_map/all_to_all | solution.py:16
  316.5 5.3 all-to-all-start.3
  321.8 0.0 all-gather.2.cloned.1.call-start
  321.8 0.7 all-gather.2.cloned.1.call-update
  322.5 4.4 copy.72
  326.9 2.7 copy.71
  329.7 4.3 gather_fusion.2
  334.0 2.4 gather_fusion.3
  336.4 5.5 broadcast_select_fusion
  341.9 15.8 %all-to-all-done.3 = bf16[8,3,128,256]{3,2,1,0:T(8,128)(2,1)} async-done(((bf16[8,3,128,256]{3,2,1,0:T(8,128)(2,1)}), bf16[8,3,128,256]{3,2,1,0:T(8,128)(2,1)}, u32[]{:S(2)}, u32[]{:S(2)}) %all-to-all-start.3) | async-done | bytes 1572896 | tf_op jit(solution)/shard_map/all_to_all | solution.py:10
  357.7 74.6 %all_to_all.118 = f32[8,3,128,256]{3,2,1,0:T(8,128)} all-to-all(f32[8,3,128,256]{3,2,1,0:T(8,128)S(1)} %get-tuple-element.6), channel_id=1, replica_groups=mesh['dp'=4,'expert'=8] {'expert'}, dimensions={0} | all-to-all | bytes 6291456 | tf_op jit(solution)/shard_map/all_to_all | solution.py:20
  432.3 4.3 all-to-all-start.7
  436.5 0.0 all-gather.2.cloned.1.call-done
  436.5 7.0 %fusion.2 = f32[1152,1024]{1,0:T(8,128)} fusion(bf16[1152,1024]{1,0:T(8,128)(2,1)} %bitcast.5, bf16[1,3,1024,1024]{3,2,1,0:T(8,128)(2,1)} %all-gather.2.cloned.1.call-done), kind=kOutput, calls=%fused_computation.16 | convolution fusion | flops 2415919104 | bytes 9175040 | tf_op jit(solution)/shard_map/dot_general | solution.py:57
  443.6 10.8 %convolution_convert_fusion = bf16[1152,1024]{1,0:T(8,128)(2,1)} fusion(bf16[1,3,1024,1024]{3,2,1,0:T(8,128)(2,1)} %all-gather.2.cloned.1.call-done, bf16[1152,1024]{1,0:T(8,128)(2,1)} %bitcast.5, f32[1152,1024]{1,0:T(8,128)} %fusion.2), kind=kOutput, calls=%fused_computation.5 | convolution fusion | flops 4840095744 | bytes 13631488 | tf_op jit(solution)/shard_map/rh,dh->rd/dot_general | solution.py:60
  454.3 51.7 %all-to-all-done.7 = f32[8,3,128,256]{3,2,1,0:T(8,128)S(1)} async-done(((f32[8,3,128,256]{3,2,1,0:T(8,128)}), f32[8,3,128,256]{3,2,1,0:T(8,128)S(1)}, u32[]{:S(2)}, u32[]{:S(2)}) %all-to-all-start.7) | async-done | bytes 3145760 | tf_op jit(solution)/shard_map/all_to_all | solution.py:21
  506.1 1.7 copy-done.3
  507.7 5.0 all-to-all-start.1
  512.7 0.1 copy.49
  512.9 2.9 copy.53
  515.8 0.0 copy-done.2
  515.8 2.0 copy.57
  517.8 1.0 copy-done.4
  518.8 2.0 copy.61
  520.8 45.1 %all-to-all-done.1 = bf16[8,144,1024]{2,1,0:T(8,128)(2,1)S(1)} async-done(((bf16[8,144,1024]{2,1,0:T(8,128)(2,1)}), bf16[8,144,1024]{2,1,0:T(8,128)(2,1)S(1)}, u32[]{:S(2)}, u32[]{:S(2)}) %all-to-all-start.1) | async-done | bytes 2359328 | tf_op jit(solution)/shard_map/all_to_all | solution.py:64
  565.9 3.6 gather_fusion
  569.5 2.5 gather.14
  572.0 3.9 multiply_reduce_fusion
  (20 shorter events, 0.1 us)
Async XLA Ops:
  7.2 14.0 %copy-start = (bf16[192,1024]{1,0:T(8,128)(2,1)S(1)}, bf16[192,1024]{1,0:T(8,128)(2,1)}, u32[]{:S(2)}) copy-start(bf16[192,1024]{1,0:T(8,128)(2,1)} %param.10) | copy-start | bytes 1179652
  7.2 10.5 %copy-start.7 = (s32[192,4]{0,1:T(4,128)S(1)}, s32[192,4]{0,1:T(4,128)}, u32[]{:S(2)}) copy-start(s32[192,4]{0,1:T(4,128)} %param.11) | copy-start | bytes 9220
  7.2 10.8 %copy-start.9 = (s32[8]{0:T(128)S(1)}, s32[8]{0:T(128)}, u32[]{:S(2)}) copy-start(s32[8]{0:T(128)} %param.13) | copy-start | bytes 100
  11.3 53.8 %all-to-all-start.2 = ((bf16[1,3,1024,256]{3,1,0,2:T(4,128)(2,1)}), bf16[1,3,1024,256]{3,1,0,2:T(4,128)(2,1)S(1)}, u32[]{:S(2)}, u32[]{:S(2)}) async-start(bf16[1,3,1024,256]{3,1,0,2:T(4,128)(2,1)} %copy.50), calls=%async_computation.2 | async-start | bytes 4194304 | tf_op jit(solution)/shard_map/all_to_all | solution.py:8
  20.4 44.7 %copy-start.5 = (s32[192,4]{1,0:T(8,128)}, s32[192,4]{1,0:T(8,128)S(1)}, u32[]{:S(2)}) copy-start(s32[192,4]{1,0:T(8,128)S(1)} %add.71) | copy-start | bytes 9220
  65.1 57.3 %all-to-all-start = ((bf16[8,144,1024]{2,1,0:T(8,128)(2,1)}), bf16[8,144,1024]{2,1,0:T(8,128)(2,1)}, u32[]{:S(2)}, u32[]{:S(2)}) async-start(bf16[8,144,1024]{2,1,0:T(8,128)(2,1)} %bitcast.4), calls=%async_computation | async-start | bytes 4718592 | tf_op jit(solution)/shard_map/all_to_all | solution.py:54
  122.5 96.9 %all-to-all-start.4 = ((f32[1,3,1024,256]{3,1,0,2:T(4,128)}), f32[1,3,1024,256]{3,1,0,2:T(4,128)}, u32[]{:S(2)}, u32[]{:S(2)}) async-start(f32[1,3,1024,256]{3,1,0,2:T(4,128)} %copy.54), calls=%async_computation.4 | async-start | bytes 8388608 | tf_op jit(solution)/shard_map/all_to_all | solution.py:15
  133.6 91.0 %copy-start.10 = (s32[8]{0:T(128)S(1)}, s32[8]{0:T(128)}, u32[]{:S(2)}) copy-start(s32[8]{0:T(128)} %param.14) | copy-start | bytes 100
  219.4 97.1 %all-to-all-start.6 = ((f32[1,3,1024,256]{3,1,0,2:T(4,128)}), f32[1,3,1024,256]{3,1,0,2:T(4,128)}, u32[]{:S(2)}, u32[]{:S(2)}) async-start(f32[1,3,1024,256]{3,1,0,2:T(4,128)} %copy.58), calls=%async_computation.6 | async-start | bytes 8388608 | tf_op jit(solution)/shard_map/all_to_all | solution.py:16
  316.5 41.2 %all-to-all-start.3 = ((bf16[8,3,128,256]{3,2,1,0:T(8,128)(2,1)}), bf16[8,3,128,256]{3,2,1,0:T(8,128)(2,1)}, u32[]{:S(2)}, u32[]{:S(2)}) async-start(bf16[8,3,128,256]{3,2,1,0:T(8,128)(2,1)} %broadcast_select_fusion.2), calls=%async_computation.3 | async-start | bytes 3145728 | tf_op jit(solution)/shard_map/all_to_all | solution.py:10
  321.8 114.8 %all-gather.2.cloned.1.call-start = ((), (), s32[]{:S(2)}) async-start(), calls=%async_computation.8 | async-start | bytes 7864320 | tf_op jit(solution)/shard_map/all_gather | solution.py:56
  432.3 73.8 %all-to-all-start.7 = ((f32[8,3,128,256]{3,2,1,0:T(8,128)}), f32[8,3,128,256]{3,2,1,0:T(8,128)S(1)}, u32[]{:S(2)}, u32[]{:S(2)}) async-start(f32[8,3,128,256]{3,2,1,0:T(8,128)} %get-tuple-element.5), calls=%async_computation.7 | async-start | bytes 6291456 | tf_op jit(solution)/shard_map/all_to_all | solution.py:21
  454.3 58.4 %copy-start.8 = (f32[192,4]{0,1:T(4,128)S(1)}, f32[192,4]{0,1:T(4,128)}, u32[]{:S(2)}) copy-start(f32[192,4]{0,1:T(4,128)} %param.12) | copy-start | bytes 9220
  454.3 58.6 %copy-start.6 = (s32[192,4]{1,0:T(8,128)S(1)}, s32[192,4]{1,0:T(8,128)}, u32[]{:S(2)}) copy-start(s32[192,4]{1,0:T(8,128)} %copy-done.5) | copy-start | bytes 9220
  506.1 1.7 copy-start.3
  507.7 58.2 %all-to-all-start.1 = ((bf16[8,144,1024]{2,1,0:T(8,128)(2,1)}), bf16[8,144,1024]{2,1,0:T(8,128)(2,1)S(1)}, u32[]{:S(2)}, u32[]{:S(2)}) async-start(bf16[8,144,1024]{2,1,0:T(8,128)(2,1)} %bitcast.71), calls=%async_computation.1 | async-start | bytes 4718592 | tf_op jit(solution)/shard_map/all_to_all | solution.py:64
  512.8 3.0 copy-start.2
  515.8 3.0 copy-start.4
  565.9 10.0 %copy-start.1 = (bf16[192,1024]{1,0:T(8,128)(2,1)S(1)}, bf16[192,1024]{1,0:T(8,128)(2,1)}, u32[]{:S(2)}) copy-start(bf16[192,1024]{1,0:T(8,128)(2,1)} %param.10) | copy-start | bytes 1179652
Sparse Core Ops, SparseCore 0:
  324.1 49.6 all-gather.1
where the time goes:
time: 585 us; the launch traced here: 583 us
  waiting for transfers between devices  374 us (64%)
  blocking collectives  74.6 us (13%)
  local copies, waits for them, and re-layouts  50 us (9%)
  starting transfers between devices  35.9 us (6%)
  matrix products  20 us (3%)
  between operations  14.3 us (2%)
  other arithmetic  13.7 us (2%)
    all_to_all x1, waiting for transfers between devices, relocate_moments(): lax.all_to_all(second_moment, 'expert', split_axis=2, concat_axis=0, tile...  86.8 us
    all_to_all x1, waiting for transfers between devices, relocate_moments(): lax.all_to_all(first_moment, 'expert', split_axis=2, concat_axis=0, tiled...  85.7 us
    all_to_all x1, blocking collectives, relocate_moments(): lax.all_to_all(ordered[0], 'expert', split_axis=0, concat_axis=2, tiled=T...  74.6 us
    all_to_all x1, waiting for transfers between devices, relocate_moments(): lax.all_to_all(ordered[1], 'expert', split_axis=0, concat_axis=2, tiled=T...  51.7 us
    all_to_all x1, waiting for transfers between devices, per_device(): lax.all_to_all(outgoing, 'expert', split_axis=0, concat_axis=0, tiled=True)  46.7 us
    all_to_all x1, waiting for transfers between devices, per_device(): lax.all_to_all(answers, 'expert', split_axis=0, concat_axis=0, tiled=True)  45.1 us
    all_to_all x1, waiting for transfers between devices, relocate_weights(): lax.all_to_all(weights, 'expert', split_axis=2, concat_axis=0, tiled=True)  41.7 us
    unnamed x27, local copies, waits for them, and re-layouts  19.2 us
  transfers between devices with their start and end apart: 8, of which 7 were waited for; matrix products, arithmetic and copies ran while one was open for 11% of the time, Pallas kernels for 0%

commit v1 on v0

v1 whole, which is shorter than its diff:
```python
import functools
import itertools

import jax
import jax.numpy as jnp
from jax import lax
from jax.experimental import pallas as pl
from jax.experimental.pallas import tpu as pltpu
from jax.sharding import PartitionSpec as P

LANES = 128
PAIR_LIMIT = 64


def ring_pairs(count):
    order = list(range(0, count, 2)) + list(range(1, count, 2))[::-1]
    ahead = [(order[i], order[(i + 1) % count]) for i in range(count)]
    return ahead, [(b, a) for a, b in ahead]


def relay_of(source, target, count):
    if source ^ 1 != target:
        return source ^ 1
    beyond = target + 2
    return beyond if beyond < count else target - 2


def swap_slots(pair, dp_count, count, payload):
    low, high = pair
    low_relay, high_relay = relay_of(low, high, count), relay_of(high, low, count)

    def spread(core, edges):
        return [
            (row * count + a, row * count + b) for row in range(core, dp_count, 2) for a, b in edges
        ]

    direct = spread(0, [(low, high), (high, low)])
    first_hop = spread(1, [(low, low_relay), (high, high_relay)])
    second_hop = spread(1, [(low_relay, high), (high_relay, low)])
    axes = ("dp", "expert")
    first = [lax.ppermute(block, axes, direct + first_hop) for block in payload]
    return tuple((block, lax.ppermute(block, axes, second_hop)) for block in first)


def any_permutation(source_slot, payload):
    count = lax.axis_size("expert")
    moved = []
    for block in payload:
        rows = block.reshape(count, -1, block.shape[3])
        spread = lax.all_to_all(rows, "expert", split_axis=0, concat_axis=0, tiled=True)
        ordered = jnp.take(spread, source_slot, axis=0)
        back = lax.all_to_all(ordered, "expert", split_axis=0, concat_axis=0, tiled=True)
        back = back.reshape(block.shape)
        moved.append((back, back))
    return tuple(moved)


def relocate(arrays, old_owner, new_owner, source_slot, dp_count, count):
    payload = tuple(a.astype(jnp.bfloat16) for a in arrays)
    pairs = list(itertools.combinations(range(count), 2))
    if len(pairs) > PAIR_LIMIT:
        moved = any_permutation(source_slot, payload)
    else:
        differs = old_owner != new_owner
        low = jnp.min(jnp.where(differs, old_owner, count))
        high = jnp.max(jnp.where(differs, old_owner, 0))
        number = low * count - low * (low + 1) // 2 + high - low - 1
        branch = jnp.where(jnp.sum(differs.astype(jnp.int32)) == 2, number, len(pairs))
        branches = [
            functools.partial(lambda pair, *p: swap_slots(pair, dp_count, count, p), pair)
            for pair in pairs
        ] + [lambda *p: any_permutation(source_slot, p)]
        moved = lax.switch(branch, branches, *payload)
    slot = lax.axis_index("expert")
    here = jnp.sum(jnp.where(jnp.arange(count) == slot, source_slot, 0)) != slot
    odd = lax.axis_index("dp") % 2 == 1
    return tuple(
        jnp.where(here, jnp.where(odd, relayed, direct).astype(own.dtype), own)
        for own, (direct, relayed) in zip(arrays, moved)
    )


def expert_kernel(blocks, shards, width, count, slot_ref, *refs):
    rows_refs, weight_refs, out_refs = (
        refs[:blocks],
        refs[blocks : blocks + shards],
        refs[blocks + shards :],
    )
    rows = jnp.concatenate([r[:, :width] for r in rows_refs], axis=0)
    extra = jnp.concatenate([r[:, width:] for r in rows_refs], axis=0).astype(jnp.float32)
    lane = lax.broadcasted_iota(jnp.int32, extra.shape, 1)
    slot = slot_ref[0]
    mine = (lane == slot) | (lane == slot + count)
    gate = jnp.sum(jnp.where(mine, extra, 0.0), axis=1, keepdims=True)
    total = None
    for w in weight_refs:
        g = jnp.dot(rows, w[0, 0], preferred_element_type=jnp.float32)
        u = jnp.dot(rows, w[0, 1], preferred_element_type=jnp.float32)
        hidden = (g / (1.0 + jnp.exp(-g)) * u).astype(jnp.bfloat16)
        part = lax.dot_general(
            hidden, w[0, 2], (((1,), (1,)), ((), ())), preferred_element_type=jnp.float32
        )
        total = part if total is None else total + part
    result = (total * gate).astype(jnp.bfloat16)
    start = 0
    for out in out_refs:
        out[...] = result[start : start + out.shape[0]]
        start += out.shape[0]


def run_expert(slot, row_blocks, shards, width, count):
    blocks = len(row_blocks)
    whole = pl.BlockSpec(memory_space=pltpu.VMEM)
    rows = sum(b.shape[0] for b in row_blocks)
    hidden = sum(s.shape[3] for s in shards)
    return pl.pallas_call(
        functools.partial(expert_kernel, blocks, len(shards), width, count),
        out_shape=[jax.ShapeDtypeStruct((b.shape[0], width), jnp.bfloat16) for b in row_blocks],
        in_specs=[pl.BlockSpec(memory_space=pltpu.SMEM)] + [whole] * (blocks + len(shards)),
        out_specs=[whole] * blocks,
        cost_estimate=pl.CostEstimate(
            flops=6 * rows * width * hidden,
            bytes_accessed=6 * width * hidden + 4 * rows * width,
            transcendentals=rows * hidden,
        ),
    )(slot, *row_blocks, *shards)


def gather_weights(weights, dp_count):
    chips = dp_count // 2
    swap = [(i, i ^ 1) for i in range(dp_count)]
    shards = [weights, lax.ppermute(weights, "dp", swap)]
    for step in range(1, chips):
        turn = [(i, (i + 2 * step) % dp_count) for i in range(dp_count)]
        far = lax.ppermute(weights, "dp", turn)
        shards += [far, lax.ppermute(far, "dp", swap)]
    return shards


def per_device(
    tokens, route_ids, gate_weight, old_owner, new_owner, weights, first_moment, second_moment
):
    count, dp_count = lax.axis_size("expert"), lax.axis_size("dp")
    tok_rows, width = tokens.shape
    labels = jnp.arange(count, dtype=jnp.int32)
    source_slot = jnp.sum(
        jnp.where(new_owner[None, :] == labels[:, None], old_owner[None, :], 0), axis=1
    )
    slot = lax.axis_index("expert").astype(jnp.int32).reshape(1)

    shards = gather_weights(weights, dp_count)

    by_expert = jnp.sum(
        jnp.where(route_ids[:, :, None] == labels[None, None, :], gate_weight[:, :, None], 0.0),
        axis=1,
    )
    by_slot = jnp.sum(
        jnp.where(old_owner[None, None, :] == labels[None, :, None], by_expert[:, None, :], 0.0),
        axis=2,
    )
    high = by_slot.astype(jnp.bfloat16)
    low = (by_slot - high.astype(jnp.float32)).astype(jnp.bfloat16)
    spare = -(-2 * count // LANES) * LANES - 2 * count
    packed = jnp.concatenate([tokens, high, low, jnp.zeros((tok_rows, spare), jnp.bfloat16)], axis=1)

    ahead, behind = ring_pairs(count)
    steps = count // 2
    half = tok_rows // 2
    from_behind, from_ahead = [packed], [packed]
    for step in range(1, steps):
        from_behind.append(lax.ppermute(from_behind[-1], "expert", ahead))
        from_ahead.append(lax.ppermute(from_ahead[-1], "expert", behind))
    far_first = lax.ppermute(from_behind[-1][:half], "expert", ahead)
    far_second = lax.ppermute(from_ahead[-1][half:], "expert", behind)

    moved_weights, moved_first, moved_second = relocate(
        (weights, first_moment, second_moment), old_owner, new_owner, source_slot, dp_count, count
    )

    apply = functools.partial(run_expert, slot, shards=shards, width=width, count=count)
    own, *near = apply([packed] + [b for b in (from_behind[1], from_ahead[1])])
    answers = {1: near}
    for step in range(2, steps):
        answers[step] = apply([from_behind[step], from_ahead[step]])
    top, bottom = apply([far_first, far_second])

    def add(a, b):
        return (a.astype(jnp.float32) + b.astype(jnp.float32)).astype(jnp.bfloat16)

    to_behind = lax.ppermute(top, "expert", behind)
    to_ahead = lax.ppermute(bottom, "expert", ahead)
    for step in range(steps - 1, 0, -1):
        back, front = answers[step]
        if step == steps - 1:
            back = jnp.concatenate([add(back[:half], to_behind), back[half:]], axis=0)
            front = jnp.concatenate([front[:half], add(front[half:], to_ahead)], axis=0)
        else:
            back, front = add(back, to_behind), add(front, to_ahead)
        to_behind = lax.ppermute(back, "expert", behind)
        to_ahead = lax.ppermute(front, "expert", ahead)
    layer_output = (
        own.astype(jnp.float32) + to_behind.astype(jnp.float32) + to_ahead.astype(jnp.float32)
    ).astype(jnp.bfloat16)
    return (layer_output, moved_weights, moved_first, moved_second)


def solution(mesh):
    placed = (
        P(("dp", "expert"), None),
        P(("dp", "expert"), None),
        P(("dp", "expert"), None),
        P(),
        P(),
        P("expert", None, None, "dp"),
        P("expert", None, None, "dp"),
        P("expert", None, None, "dp"),
    )
    return jax.shard_map(
        per_device,
        mesh=mesh,
        in_specs=placed,
        out_specs=(
            P(("dp", "expert"), None),
            P("expert", None, None, "dp"),
            P("expert", None, None, "dp"),
            P("expert", None, None, "dp"),
        ),
        check_vma=False,
    )
```

time: 585 us -> 242 us (0.41)
  waiting for transfers between devices: 374 us -> 56.7 us
  starting transfers between devices: 35.9 us -> 125 us
  blocking collectives: 74.6 us -> 0 us
  local copies, waits for them, and re-layouts: 50 us -> 6.42 us
  Pallas kernels: 0 us -> 25.3 us
  matrix products: 20 us -> 0 us
  other arithmetic: 13.7 us -> 24.5 us
  between operations: 14.3 us -> 5.47 us
    all_to_all x7 -> x0, waiting for transfers between devices: 374 us -> none  [the longest x1 86.8 us: relocate_moments(): lax.all_to_all(second_moment, 'expert', split_axis=2, concat_axis=0, tile...]
    ppermute x0 -> x25, starting transfers between devices: none -> 125 us  [the longest x3 44.5 us: swap_slots(): lax.ppermute(block, axes, second_hop)]
    all_to_all x1 -> x0, blocking collectives: 74.6 us -> none  [relocate_moments(): lax.all_to_all(ordered[0], 'expert', split_axis=0, concat_axis=2, tiled=T...]
    ppermute x0 -> x25, waiting for transfers between devices: none -> 56.7 us  [the longest x1 27.5 us: gather_weights(): far = lax.ppermute(weights, 'dp', turn)]
    all_to_all x7 -> x0, starting transfers between devices: 35.9 us -> none  [the longest x1 6.37 us: relocate_weights(): lax.all_to_all(weights, 'expert', split_axis=2, concat_axis=0, tiled=True)]
    pallas_call x0 -> x4, Pallas kernels: none -> 25.3 us  [run_expert(): pl.pallas_call(functools.partial(expert_kernel, blocks, len(shards), widt...]
    dot_general x3 -> x0, matrix products: 20 us -> none  [the longest x1 10.8 us: per_device(): jnp.einsum('rh,dh->rd', hidden, shard_piece[0, 2], preferred_element_type...]
    unnamed x27 -> x30, local copies, waits for them, and re-layouts: 19.2 us -> 2.01 us
  transfers between devices with their start and end apart: 8 -> 25, of which waited for: 7 -> 12; matrix products, arithmetic and copies ran while one was open for 11% -> 11% of each run, Pallas kernels for 0% -> 8%
where the time goes in v1:
time: 242 us; the launch traced here: 244 us
  starting transfers between devices  125 us (52%)
  waiting for transfers between devices  56.7 us (23%)
  Pallas kernels  25.3 us (10%)
  other arithmetic  24.5 us (10%)
  local copies, waits for them, and re-layouts  6.42 us (3%)
  between operations  5.47 us (2%)
    ppermute x3, starting transfers between devices, swap_slots(): lax.ppermute(block, axes, second_hop)  44.5 us
    ppermute x3, starting transfers between devices, per_device(): from_behind.append(lax.ppermute(from_behind[-1], 'expert', ahead))  30.5 us
    ppermute x1, waiting for transfers between devices, gather_weights(): far = lax.ppermute(weights, 'dp', turn)  27.5 us
    pallas_call x4, Pallas kernels, run_expert(): pl.pallas_call(functools.partial(expert_kernel, blocks, len(shards), widt...  25.3 us
    ppermute x3, starting transfers between devices, swap_slots(): first = [lax.ppermute(block, axes, direct + first_hop) for block in payload]  22.8 us
    ppermute x3, waiting for transfers between devices, per_device(): from_behind.append(lax.ppermute(from_behind[-1], 'expert', ahead))  22.1 us
    select_n x2, other arithmetic, relocate(): jnp.where(here, jnp.where(odd, relayed, direct).astype(own.dtype), own)  10.2 us
    ppermute x1, starting transfers between devices, gather_weights(): far = lax.ppermute(weights, 'dp', turn)  7.04 us
  transfers between devices with their start and end apart: 25, of which 12 were waited for; matrix products, arithmetic and copies ran while one was open for 11% of the time, Pallas kernels for 8%

profile of v1, /device:TPU:1, one launch (start us, length us, event | category | flops | bytes accessed | tf_op | source)
XLA Modules:
  0.0 243.9 jit_solution(5173754770247015849)
XLA Ops:
  0.6 7.0 %collective-permute-start.171 = (bf16[1,3,1024,256]{3,2,1,0:T(8,128)(2,1)}, bf16[1,3,1024,256]{3,2,1,0:T(8,128)(2,1)}, u32[]{:S(2)}, u32[]{:S(2)}) collective-permute-start(bf16[1,3,1024,256]{3,2,1,0:T(8,128)(2,1)} %refs_2_.5), channel_id=1, source_target_pairs={{0,16},{8,24},{16,0},{24,8},{1,17},{9,25},{17,1},{25,9},{2,18},{10... | collective-permute-start | bytes 4718600 | tf_op jit(solution)/shard_map/ppermute | solution.py:135
  7.7 5.7 %collective-permute-start.170 = (bf16[1,3,1024,256]{3,2,1,0:T(8,128)(2,1)}, bf16[1,3,1024,256]{3,2,1,0:T(8,128)(2,1)}, u32[]{:S(2)}, u32[]{:S(2)}) collective-permute-start(bf16[1,3,1024,256]{3,2,1,0:T(8,128)(2,1)} %refs_2_.5), channel_id=1, source_target_pairs={{0,8},{8,0},{16,24},{24,16},{1,9},{9,1},{17,25},{25,17},{2,10},{10... | collective-permute-start | bytes 4718600 | tf_op jit(solution)/shard_map/ppermute | solution.py:132
  13.4 1.3 select_reduce_fusion.3
  14.7 0.7 select_reduce_fusion.1
  15.5 0.7 iota_compare_fusion.2
  16.1 0.1 select_reduce_fusion
  16.2 27.5 %collective-permute-done.171.refs_5_.refs_4_ = bf16[1,3,1024,256]{3,2,1,0:T(8,128)(2,1)} collective-permute-done((bf16[1,3,1024,256]{3,2,1,0:T(8,128)(2,1)}, bf16[1,3,1024,256]{3,2,1,0:T(8,128)(2,1)}, u32[]{:S(2)}, u32[]{:S(2)}) %collective-permute-start.171) | collective-permute-done | bytes 1572896 | tf_op jit(solution)/shard_map/ppermute | solution.py:135
  43.7 5.2 %collective-permute-start.172 = (bf16[1,3,1024,256]{3,2,1,0:T(8,128)(2,1)}, bf16[1,3,1024,256]{3,2,1,0:T(8,128)(2,1)}, u32[]{:S(2)}, u32[]{:S(2)}) collective-permute-start(bf16[1,3,1024,256]{3,2,1,0:T(8,128)(2,1)} %collective-permute-done.171.refs_5_.refs_4_), channel_id=1, source_target_pairs={{0,8},{8,0},{16,24},{24,16},{1,9},{9,1},{17,25},{25,17},{2,10},{10... | collective-permute-start | bytes 4718600 | tf_op jit(solution)/shard_map/ppermute | solution.py:136
  49.0 0.8 select_reduce_fusion.2
  53.7 2.2 convert_element_type.116
  55.9 0.6 copy-done.1
  56.5 1.3 convert_element_type.117
  57.8 0.7 copy.14
  58.5 0.7 copy.15
  59.3 67.6 %conditional.1 = (bf16[1,3,1024,256]{3,2,1,0:T(8,128)(2,1)}, bf16[1,3,1024,256]{3,2,1,0:T(8,128)(2,1)}, bf16[1,3,1024,256]{3,2,1,0:T(8,128)(2,1)}, bf16[1,3,1024...) conditional(s32[]{:T(128)} %clamp.3, ...), branch_computations={%region_7.8_spmd, %region_8.9_spmd, %region_9.10_spmd, %region_10.... | conditional | flops 2360392 | bytes 50336096 | solution.py:73
  59.3 7.7 %collective-permute-start.150 = (bf16[1,3,1024,256]{3,2,1,0:T(8,128)(2,1)S(1)}, bf16[1,3,1024,256]{3,2,1,0:T(8,128)(2,1)}, u32[]{:S(2)}, u32[]{:S(2)}) collective-permute-start(bf16[1,3,1024,256]{3,2,1,0:T(8,128)(2,1)S(1)} %get-tuple-element.252), channel_id=1, source_target_pairs={{5,6},{6,5},{21,22},{22,21},{13,12},{14,15},{29,28},{30,31}} | collective-permute-start | bytes 4718600 | tf_op jit(solution)/shard_map/cond/branch_25_fun/ppermute | solution.py:41
  67.0 7.5 %collective-permute-start.152 = (bf16[1,3,1024,256]{3,2,1,0:T(8,128)(2,1)S(1)}, bf16[1,3,1024,256]{3,2,1,0:T(8,128)(2,1)}, u32[]{:S(2)}, u32[]{:S(2)}) collective-permute-start(bf16[1,3,1024,256]{3,2,1,0:T(8,128)(2,1)S(1)} %get-tuple-element.253), channel_id=1, source_target_pairs={{5,6},{6,5},{21,22},{22,21},{13,12},{14,15},{29,28},{30,31}} | collective-permute-start | bytes 4718600 | tf_op jit(solution)/shard_map/cond/branch_25_fun/ppermute | solution.py:41
  74.6 7.5 %collective-permute-start.154 = (bf16[1,3,1024,256]{3,2,1,0:T(8,128)(2,1)}, bf16[1,3,1024,256]{3,2,1,0:T(8,128)(2,1)}, u32[]{:S(2)}, u32[]{:S(2)}) collective-permute-start(bf16[1,3,1024,256]{3,2,1,0:T(8,128)(2,1)} %get-tuple-element.254), channel_id=1, source_target_pairs={{5,6},{6,5},{21,22},{22,21},{13,12},{14,15},{29,28},{30,31}} | collective-permute-start | bytes 4718600 | tf_op jit(solution)/shard_map/cond/branch_25_fun/ppermute | solution.py:41
  82.1 10.8 %collective-permute-start.151 = (bf16[1,3,1024,256]{3,2,1,0:T(8,128)(2,1)}, bf16[1,3,1024,256]{3,2,1,0:T(8,128)(2,1)}, u32[]{:S(2)}, u32[]{:S(2)}) collective-permute-start(bf16[1,3,1024,256]{3,2,1,0:T(8,128)(2,1)} %collective-permute-done.150), channel_id=1, source_target_pairs={{12,14},{15,13},{28,30},{31,29}} | collective-permute-start | bytes 4718600 | tf_op jit(solution)/shard_map/cond/branch_25_fun/ppermute | solution.py:42
  92.9 16.9 %collective-permute-start.153 = (bf16[1,3,1024,256]{3,2,1,0:T(8,128)(2,1)}, bf16[1,3,1024,256]{3,2,1,0:T(8,128)(2,1)}, u32[]{:S(2)}, u32[]{:S(2)}) collective-permute-start(bf16[1,3,1024,256]{3,2,1,0:T(8,128)(2,1)} %collective-permute-done.152), channel_id=1, source_target_pairs={{12,14},{15,13},{28,30},{31,29}} | collective-permute-start | bytes 4718600 | tf_op jit(solution)/shard_map/cond/branch_25_fun/ppermute | solution.py:42
  109.8 16.8 %collective-permute-start.155 = (bf16[1,3,1024,256]{3,2,1,0:T(8,128)(2,1)}, bf16[1,3,1024,256]{3,2,1,0:T(8,128)(2,1)}, u32[]{:S(2)}, u32[]{:S(2)}) collective-permute-start(bf16[1,3,1024,256]{3,2,1,0:T(8,128)(2,1)} %collective-permute-done.154), channel_id=1, source_target_pairs={{12,14},{15,13},{28,30},{31,29}} | collective-permute-start | bytes 4718600 | tf_op jit(solution)/shard_map/cond/branch_25_fun/ppermute | solution.py:42
  126.9 1.0 concatenate.9.refs_0_
  127.9 1.4 collective-permute-start.168
  129.3 0.1 collective-permute-start.169
  129.4 10.1 %collective-permute-done.168.refs_1_ = bf16[192,1152]{1,0:T(8,128)(2,1)S(1)} collective-permute-done((bf16[192,1152]{1,0:T(8,128)(2,1)S(1)}, bf16[192,1152]{1,0:T(8,128)(2,1)S(1)}, u32[]{:S(2)}, u32[]{:S(2)}) %collective-permute-start.168) | collective-permute-done | bytes 442400 | tf_op jit(solution)/shard_map/ppermute | solution.py:171
  139.5 26.9 %collective-permute-start.173 = (bf16[192,1152]{1,0:T(8,128)(2,1)S(1)}, bf16[192,1152]{1,0:T(8,128)(2,1)S(1)}, u32[]{:S(2)}, u32[]{:S(2)}) collective-permute-start(bf16[192,1152]{1,0:T(8,128)(2,1)S(1)} %collective-permute-done.168.refs_1_), channel_id=1, source_target_pairs={{0,2},{2,4},{4,6},{6,7},{7,5},{5,3},{3,1},{1,0},{8,10},{10,12},{12... | collective-permute-start | bytes 1327112 | tf_op jit(solution)/shard_map/ppermute | solution.py:171
  166.4 0.4 collective-permute-done.169.refs_2_
  166.9 7.2 %collective-permute-done.173.refs_0_ = bf16[192,1152]{1,0:T(8,128)(2,1)S(1)} collective-permute-done((bf16[192,1152]{1,0:T(8,128)(2,1)S(1)}, bf16[192,1152]{1,0:T(8,128)(2,1)S(1)}, u32[]{:S(2)}, u32[]{:S(2)}) %collective-permute-start.173) | collective-permute-done | bytes 442400 | tf_op jit(solution)/shard_map/ppermute | solution.py:171
  174.1 2.2 collective-permute-start.175
  176.3 1.0 collective-permute-done.174.refs_1_
  177.3 4.8 %collective-permute-done.175.refs_0_ = bf16[192,1152]{1,0:T(8,128)(2,1)S(1)} collective-permute-done((bf16[192,1152]{1,0:T(8,128)(2,1)S(1)}, bf16[192,1152]{1,0:T(8,128)(2,1)S(1)}, u32[]{:S(2)}, u32[]{:S(2)}) %collective-permute-start.175) | collective-permute-done | bytes 442400 | tf_op jit(solution)/shard_map/ppermute | solution.py:171
  182.1 1.7 collective-permute-start.177
  183.8 0.9 collective-permute-done.176.refs_1_
  184.7 0.1 collective-permute-start.178
  184.8 0.7 copy-done.9
  185.5 0.6 fusion
  186.7 1.0 collective-permute-done.177.refs_0_
  187.8 2.0 collective-permute-done.178.refs_1_
  189.8 0.7 copy-done.7
  190.5 5.1 %shard_map.114 = (bf16[96,1024]{1,0:T(8,128)(2,1)}, bf16[96,1024]{1,0:T(8,128)(2,1)}) custom-call(s32[1]{0:T(128)} %bitcast.6.slot_ref, bf16[96,1152]{1,0:T(8,128)(2,1)} %copy-done.6, bf16[96,1152]{1,0:T(8,128)(2,1)} %copy-done.7, bf16[1,3,1024,256]{3,2,1,0:T(8,128)(2,1)S(1)} %copy-done, bf16[1,3,1024,256]{3,2,1,0:T(8,128)(2,1)} %collective-permute-done.170.refs_4_.refs_3_, ...), custom_call_target="tpu_custom_call" | custom-call | flops 1207959552 | bytes 7077888 | tf_op jit(solution)/shard_map/pallas_call | solution.py:116
  195.6 0.1 collective-permute-start.179
  195.7 6.3 %shard_map.113 = (bf16[192,1024]{1,0:T(8,128)(2,1)}, bf16[192,1024]{1,0:T(8,128)(2,1)}) custom-call(s32[1]{0:T(128)} %bitcast.6.slot_ref, bf16[192,1152]{1,0:T(8,128)(2,1)} %copy-done.8, bf16[192,1152]{1,0:T(8,128)(2,1)} %copy-done.9, bf16[1,3,1024,256]{3,2,1,0:T(8,128)(2,1)S(1)} %copy-done, ...), custom_call_target="tpu_custom_call" | custom-call | flops 2415919104 | bytes 7864320 | tf_op jit(solution)/shard_map/pallas_call | solution.py:116
  202.0 1.0 slice.21
  203.0 1.8 collective-permute-start.183
  204.8 0.9 slice.22
  205.8 1.0 add_convert_fusion.6
  206.8 0.1 collective-permute-start.180
  206.9 0.7 collective-permute-done.183
  207.7 1.8 collective-permute-start.184
  209.5 6.3 %shard_map.112 = (bf16[192,1024]{1,0:T(8,128)(2,1)}, bf16[192,1024]{1,0:T(8,128)(2,1)}) custom-call(s32[1]{0:T(128)} %bitcast.6.slot_ref, bf16[192,1152]{1,0:T(8,128)(2,1)} %copy-done.12, bf16[192,1152]{1,0:T(8,128)(2,1)} %copy-done.13, bf16[1,3,1024,256]{3,2,1,0:T(8,128)(2,1)S(1)} %copy-done, ...), custom_call_target="tpu_custom_call" | custom-call | flops 2415919104 | bytes 7864320 | tf_op jit(solution)/shard_map/pallas_call | solution.py:116
  215.8 0.8 collective-permute-done.180
  216.6 1.1 add_convert_fusion.4
  217.7 0.1 collective-permute-start.181
  217.8 1.1 add_convert_fusion.2
  218.9 1.8 collective-permute-start.185
  220.7 7.5 %shard_map.111 = (bf16[192,1024]{1,0:T(8,128)(2,1)}, bf16[192,1024]{1,0:T(8,128)(2,1)}, bf16[192,1024]{1,0:T(8,128)(2,1)}) custom-call(s32[1]{0:T(128)} %bitcast.6.slot_ref, bf16[192,1152]{1,0:T(8,128)(2,1)} %copy-done.2, bf16[192,1152]{1,0:T(8,128)(2,1)} %copy-done.10, bf16[192,1152]{1,0:T(8,128)(2,1)} %copy-done.11, bf16[1,3,1024,256]{3,2,1,0:T(8,128)(2,1)S(1)} %copy-done, ...), custom_call_target="tpu_custom_call" | custom-call | flops 3623878656 | bytes 8650752 | tf_op jit(solution)/shard_map/pallas_call | solution.py:116
  228.2 0.3 collective-permute-done.181
  228.5 1.1 add_convert_fusion.3
  229.6 0.1 collective-permute-start.182
  229.7 1.1 add_convert_fusion.1
  230.8 1.8 collective-permute-start.186
  232.7 7.4 %convert_select_fusion = (f32[1,3,1024,256]{3,2,1,0:T(8,128)}, f32[1,3,1024,256]{3,2,1,0:T(8,128)}) fusion(f32[1,3,1024,256]{3,2,1,0:T(8,128)} %param.46, bf16[1,3,1024,256]{3,2,1,0:T(8,128)(2,1)} %get-tuple-element.297, bf16[1,3,1024,256]{3,2,1,0:T(8,128)(2,1)} %get-tuple-element.298, pred[]{:T(512)S(6)} %eq.69, pred[]{:T(512)S(6)} %ne.20, ...), kind=kLoop, calls=%fused_computation.9 | loop fusion | flops 4718592 | bytes 18874370 | tf_op jit(solution)/shard_map/jit(_where)/select_n | solution.py:78
  240.1 2.8 %select_select_fusion = bf16[1,3,1024,256]{3,2,1,0:T(8,128)(2,1)} fusion(bf16[1,3,1024,256]{3,2,1,0:T(8,128)(2,1)S(1)} %copy-done, bf16[1,3,1024,256]{3,2,1,0:T(8,128)(2,1)} %get-tuple-element.293, bf16[1,3,1024,256]{3,2,1,0:T(8,128)(2,1)} %get-tuple-element.294, pred[]{:T(512)S(6)} %eq.69, pred[]{:T(512)S(6)} %ne.20), kind=kLoop, calls=%fused_computation.11 | loop fusion | flops 1572864 | bytes 6291458 | tf_op jit(solution)/shard_map/jit(_where)/select_n | solution.py:78
  242.9 0.9 add_convert_fusion
  (49 shorter events, 0.3 us)
Async XLA Ops:
  0.6 43.1 %collective-permute-start.171 = (bf16[1,3,1024,256]{3,2,1,0:T(8,128)(2,1)}, bf16[1,3,1024,256]{3,2,1,0:T(8,128)(2,1)}, u32[]{:S(2)}, u32[]{:S(2)}) collective-permute-start(bf16[1,3,1024,256]{3,2,1,0:T(8,128)(2,1)} %refs_2_.5), channel_id=1, source_target_pairs={{0,16},{8,24},{16,0},{24,8},{1,17},{9,25},{17,1},{25,9},{2,18},{10... | collective-permute-start | bytes 4718600 | tf_op jit(solution)/shard_map/ppermute | solution.py:135
  7.7 182.1 %collective-permute-start.170 = (bf16[1,3,1024,256]{3,2,1,0:T(8,128)(2,1)}, bf16[1,3,1024,256]{3,2,1,0:T(8,128)(2,1)}, u32[]{:S(2)}, u32[]{:S(2)}) collective-permute-start(bf16[1,3,1024,256]{3,2,1,0:T(8,128)(2,1)} %refs_2_.5), channel_id=1, source_target_pairs={{0,8},{8,0},{16,24},{24,16},{1,9},{9,1},{17,25},{25,17},{2,10},{10... | collective-permute-start | bytes 4718600 | tf_op jit(solution)/shard_map/ppermute | solution.py:132
  43.7 146.1 %collective-permute-start.172 = (bf16[1,3,1024,256]{3,2,1,0:T(8,128)(2,1)}, bf16[1,3,1024,256]{3,2,1,0:T(8,128)(2,1)}, u32[]{:S(2)}, u32[]{:S(2)}) collective-permute-start(bf16[1,3,1024,256]{3,2,1,0:T(8,128)(2,1)} %collective-permute-done.171.refs_5_.refs_4_), channel_id=1, source_target_pairs={{0,8},{8,0},{16,24},{24,16},{1,9},{9,1},{17,25},{25,17},{2,10},{10... | collective-permute-start | bytes 4718600 | tf_op jit(solution)/shard_map/ppermute | solution.py:136
  53.7 2.8 %copy-start.1 = (f32[1,3,1024,256]{3,2,1,0:T(8,128)S(1)}, f32[1,3,1024,256]{3,2,1,0:T(8,128)}, u32[]{:S(2)}) copy-start(f32[1,3,1024,256]{3,2,1,0:T(8,128)} %param.46) | copy-start | bytes 9437188
  56.5 2.0 copy-start
  59.3 67.6 %copy-start.4 = (bf16[192,1024]{1,0:T(8,128)(2,1)S(1)}, bf16[192,1024]{1,0:T(8,128)(2,1)}, u32[]{:S(2)}) copy-start(bf16[192,1024]{1,0:T(8,128)(2,1)} %param.39) | copy-start | bytes 1179652
  59.3 22.8 %collective-permute-start.150 = (bf16[1,3,1024,256]{3,2,1,0:T(8,128)(2,1)S(1)}, bf16[1,3,1024,256]{3,2,1,0:T(8,128)(2,1)}, u32[]{:S(2)}, u32[]{:S(2)}) collective-permute-start(bf16[1,3,1024,256]{3,2,1,0:T(8,128)(2,1)S(1)} %get-tuple-element.252), channel_id=1, source_target_pairs={{5,6},{6,5},{21,22},{22,21},{13,12},{14,15},{29,28},{30,31}} | collective-permute-start | bytes 4718600 | tf_op jit(solution)/shard_map/cond/branch_25_fun/ppermute | solution.py:41
  67.0 25.9 %collective-permute-start.152 = (bf16[1,3,1024,256]{3,2,1,0:T(8,128)(2,1)S(1)}, bf16[1,3,1024,256]{3,2,1,0:T(8,128)(2,1)}, u32[]{:S(2)}, u32[]{:S(2)}) collective-permute-start(bf16[1,3,1024,256]{3,2,1,0:T(8,128)(2,1)S(1)} %get-tuple-element.253), channel_id=1, source_target_pairs={{5,6},{6,5},{21,22},{22,21},{13,12},{14,15},{29,28},{30,31}} | collective-permute-start | bytes 4718600 | tf_op jit(solution)/shard_map/cond/branch_25_fun/ppermute | solution.py:41
  74.6 35.2 %collective-permute-start.154 = (bf16[1,3,1024,256]{3,2,1,0:T(8,128)(2,1)}, bf16[1,3,1024,256]{3,2,1,0:T(8,128)(2,1)}, u32[]{:S(2)}, u32[]{:S(2)}) collective-permute-start(bf16[1,3,1024,256]{3,2,1,0:T(8,128)(2,1)} %get-tuple-element.254), channel_id=1, source_target_pairs={{5,6},{6,5},{21,22},{22,21},{13,12},{14,15},{29,28},{30,31}} | collective-permute-start | bytes 4718600 | tf_op jit(solution)/shard_map/cond/branch_25_fun/ppermute | solution.py:41
  82.1 44.5 %collective-permute-start.151 = (bf16[1,3,1024,256]{3,2,1,0:T(8,128)(2,1)}, bf16[1,3,1024,256]{3,2,1,0:T(8,128)(2,1)}, u32[]{:S(2)}, u32[]{:S(2)}) collective-permute-start(bf16[1,3,1024,256]{3,2,1,0:T(8,128)(2,1)} %collective-permute-done.150), channel_id=1, source_target_pairs={{12,14},{15,13},{28,30},{31,29}} | collective-permute-start | bytes 4718600 | tf_op jit(solution)/shard_map/cond/branch_25_fun/ppermute | solution.py:42
  92.9 33.7 %collective-permute-start.153 = (bf16[1,3,1024,256]{3,2,1,0:T(8,128)(2,1)}, bf16[1,3,1024,256]{3,2,1,0:T(8,128)(2,1)}, u32[]{:S(2)}, u32[]{:S(2)}) collective-permute-start(bf16[1,3,1024,256]{3,2,1,0:T(8,128)(2,1)} %collective-permute-done.152), channel_id=1, source_target_pairs={{12,14},{15,13},{28,30},{31,29}} | collective-permute-start | bytes 4718600 | tf_op jit(solution)/shard_map/cond/branch_25_fun/ppermute | solution.py:42
  109.8 16.9 %collective-permute-start.155 = (bf16[1,3,1024,256]{3,2,1,0:T(8,128)(2,1)}, bf16[1,3,1024,256]{3,2,1,0:T(8,128)(2,1)}, u32[]{:S(2)}, u32[]{:S(2)}) collective-permute-start(bf16[1,3,1024,256]{3,2,1,0:T(8,128)(2,1)} %collective-permute-done.154), channel_id=1, source_target_pairs={{12,14},{15,13},{28,30},{31,29}} | collective-permute-start | bytes 4718600 | tf_op jit(solution)/shard_map/cond/branch_25_fun/ppermute | solution.py:42
  127.9 67.8 %copy-start.2 = (bf16[192,1152]{1,0:T(8,128)(2,1)}, bf16[192,1152]{1,0:T(8,128)(2,1)S(1)}, u32[]{:S(2)}) copy-start(bf16[192,1152]{1,0:T(8,128)(2,1)S(1)} %concatenate.9.refs_0_) | copy-start | bytes 1327108
  127.9 11.6 %collective-permute-start.168 = (bf16[192,1152]{1,0:T(8,128)(2,1)S(1)}, bf16[192,1152]{1,0:T(8,128)(2,1)S(1)}, u32[]{:S(2)}, u32[]{:S(2)}) collective-permute-start(bf16[192,1152]{1,0:T(8,128)(2,1)S(1)} %concatenate.9.refs_0_), channel_id=1, source_target_pairs={{0,2},{2,4},{4,6},{6,7},{7,5},{5,3},{3,1},{1,0},{8,10},{10,12},{12... | collective-permute-start | bytes 1327112 | tf_op jit(solution)/shard_map/ppermute | solution.py:171
  129.3 37.6 %collective-permute-start.169 = (bf16[192,1152]{1,0:T(8,128)(2,1)S(1)}, bf16[192,1152]{1,0:T(8,128)(2,1)S(1)}, u32[]{:S(2)}, u32[]{:S(2)}) collective-permute-start(bf16[192,1152]{1,0:T(8,128)(2,1)S(1)} %concatenate.9.refs_0_), channel_id=1, source_target_pairs={{2,0},{4,2},{6,4},{7,6},{5,7},{3,5},{1,3},{0,1},{10,8},{12,10},{14... | collective-permute-start | bytes 1327112 | tf_op jit(solution)/shard_map/ppermute | solution.py:172
  139.5 37.7 %copy-start.10 = (bf16[192,1152]{1,0:T(8,128)(2,1)}, bf16[192,1152]{1,0:T(8,128)(2,1)S(1)}, u32[]{:S(2)}) copy-start(bf16[192,1152]{1,0:T(8,128)(2,1)S(1)} %collective-permute-done.168.refs_1_) | copy-start | bytes 1327108
  139.5 34.5 %collective-permute-start.173 = (bf16[192,1152]{1,0:T(8,128)(2,1)S(1)}, bf16[192,1152]{1,0:T(8,128)(2,1)S(1)}, u32[]{:S(2)}, u32[]{:S(2)}) collective-permute-start(bf16[192,1152]{1,0:T(8,128)(2,1)S(1)} %collective-permute-done.168.refs_1_), channel_id=1, source_target_pairs={{0,2},{2,4},{4,6},{6,7},{7,5},{5,3},{3,1},{1,0},{8,10},{10,12},{12... | collective-permute-start | bytes 1327112 | tf_op jit(solution)/shard_map/ppermute | solution.py:171
  166.9 10.4 %copy-start.11 = (bf16[192,1152]{1,0:T(8,128)(2,1)}, bf16[192,1152]{1,0:T(8,128)(2,1)S(1)}, u32[]{:S(2)}) copy-start(bf16[192,1152]{1,0:T(8,128)(2,1)S(1)} %collective-permute-done.169.refs_2_) | copy-start | bytes 1327108
  166.9 10.4 %collective-permute-start.174 = (bf16[192,1152]{1,0:T(8,128)(2,1)S(1)}, bf16[192,1152]{1,0:T(8,128)(2,1)S(1)}, u32[]{:S(2)}, u32[]{:S(2)}) collective-permute-start(bf16[192,1152]{1,0:T(8,128)(2,1)S(1)} %collective-permute-done.169.refs_2_), channel_id=1, source_target_pairs={{2,0},{4,2},{6,4},{7,6},{5,7},{3,5},{1,3},{0,1},{10,8},{12,10},{14... | collective-permute-start | bytes 1327112 | tf_op jit(solution)/shard_map/ppermute | solution.py:172
  174.1 8.0 %copy-start.12 = (bf16[192,1152]{1,0:T(8,128)(2,1)}, bf16[192,1152]{1,0:T(8,128)(2,1)S(1)}, u32[]{:S(2)}) copy-start(bf16[192,1152]{1,0:T(8,128)(2,1)S(1)} %collective-permute-done.173.refs_0_) | copy-start | bytes 1327108
  174.1 8.0 %collective-permute-start.175 = (bf16[192,1152]{1,0:T(8,128)(2,1)S(1)}, bf16[192,1152]{1,0:T(8,128)(2,1)S(1)}, u32[]{:S(2)}, u32[]{:S(2)}) collective-permute-start(bf16[192,1152]{1,0:T(8,128)(2,1)S(1)} %collective-permute-done.173.refs_0_), channel_id=1, source_target_pairs={{0,2},{2,4},{4,6},{6,7},{7,5},{5,3},{3,1},{1,0},{8,10},{10,12},{12... | collective-permute-start | bytes 1327112 | tf_op jit(solution)/shard_map/ppermute | solution.py:171
  177.3 7.5 %copy-start.13 = (bf16[192,1152]{1,0:T(8,128)(2,1)}, bf16[192,1152]{1,0:T(8,128)(2,1)S(1)}, u32[]{:S(2)}) copy-start(bf16[192,1152]{1,0:T(8,128)(2,1)S(1)} %collective-permute-done.174.refs_1_) | copy-start | bytes 1327108
  177.3 7.4 %collective-permute-start.176 = (bf16[192,1152]{1,0:T(8,128)(2,1)S(1)}, bf16[192,1152]{1,0:T(8,128)(2,1)S(1)}, u32[]{:S(2)}, u32[]{:S(2)}) collective-permute-start(bf16[192,1152]{1,0:T(8,128)(2,1)S(1)} %collective-permute-done.174.refs_1_), channel_id=1, source_target_pairs={{2,0},{4,2},{6,4},{7,6},{5,7},{3,5},{1,3},{0,1},{10,8},{12,10},{14... | collective-permute-start | bytes 1327112 | tf_op jit(solution)/shard_map/ppermute | solution.py:172
  182.0 13.6 %copy-start.8 = (bf16[192,1152]{1,0:T(8,128)(2,1)}, bf16[192,1152]{1,0:T(8,128)(2,1)S(1)}, u32[]{:S(2)}) copy-start(bf16[192,1152]{1,0:T(8,128)(2,1)S(1)} %collective-permute-done.175.refs_0_) | copy-start | bytes 1327108
  182.1 5.7 %collective-permute-start.177 = (bf16[96,1152]{1,0:T(8,128)(2,1)S(1)}, bf16[96,1152]{1,0:T(8,128)(2,1)S(1)}, u32[]{:S(2)}, u32[]{:S(2)}) collective-permute-start(bf16[96,1152]{1,0:T(8,128)(2,1)S(1)} %slice.30), channel_id=1, source_target_pairs={{0,2},{2,4},{4,6},{6,7},{7,5},{5,3},{3,1},{1,0},{8,10},{10,12},{12... | collective-permute-start | bytes 663560 | tf_op jit(solution)/shard_map/ppermute | solution.py:173
  184.7 0.8 copy-start.9
  184.7 5.1 %collective-permute-start.178 = (bf16[96,1152]{1,0:T(8,128)(2,1)S(1)}, bf16[96,1152]{1,0:T(8,128)(2,1)S(1)}, u32[]{:S(2)}, u32[]{:S(2)}) collective-permute-start(bf16[96,1152]{1,0:T(8,128)(2,1)S(1)} %slice.31), channel_id=1, source_target_pairs={{2,0},{4,2},{6,4},{7,6},{5,7},{3,5},{1,3},{0,1},{10,8},{12,10},{14... | collective-permute-start | bytes 663560 | tf_op jit(solution)/shard_map/ppermute | solution.py:174
  187.8 2.0 copy-start.6
  189.8 0.7 copy-start.7
  195.6 7.4 %copy-start.14 = (bf16[96,1024]{1,0:T(8,128)(2,1)S(1)}, bf16[96,1024]{1,0:T(8,128)(2,1)}, u32[]{:S(2)}) copy-start(bf16[96,1024]{1,0:T(8,128)(2,1)} %get-tuple-element.292) | copy-start | bytes 589828
  195.6 10.2 %collective-permute-start.179 = (bf16[96,1024]{1,0:T(8,128)(2,1)}, bf16[96,1024]{1,0:T(8,128)(2,1)S(1)}, u32[]{:S(2)}, u32[]{:S(2)}) collective-permute-start(bf16[96,1024]{1,0:T(8,128)(2,1)} %get-tuple-element.288), channel_id=1, source_target_pairs={{2,0},{4,2},{6,4},{7,6},{5,7},{3,5},{1,3},{0,1},{10,8},{12,10},{14... | collective-permute-start | bytes 589832 | tf_op jit(solution)/shard_map/ppermute | solution.py:190
  202.0 5.6 %copy-start.3 = (bf16[192,1024]{1,0:T(8,128)(2,1)S(1)}, bf16[192,1024]{1,0:T(8,128)(2,1)}, u32[]{:S(2)}) copy-start(bf16[192,1024]{1,0:T(8,128)(2,1)} %get-tuple-element.291) | copy-start | bytes 1179652
  203.0 4.6 %collective-permute-start.183 = (bf16[96,1024]{1,0:T(8,128)(2,1)S(1)}, bf16[96,1024]{1,0:T(8,128)(2,1)S(1)}, u32[]{:S(2)}, u32[]{:S(2)}) collective-permute-start(bf16[96,1024]{1,0:T(8,128)(2,1)S(1)} %copy-done.14), channel_id=1, source_target_pairs={{0,2},{2,4},{4,6},{6,7},{7,5},{5,3},{3,1},{1,0},{8,10},{10,12},{12... | collective-permute-start | bytes 589832 | tf_op jit(solution)/shard_map/ppermute | solution.py:191
  206.8 9.7 %collective-permute-start.180 = (bf16[192,1024]{1,0:T(8,128)(2,1)S(1)}, bf16[192,1024]{1,0:T(8,128)(2,1)S(1)}, u32[]{:S(2)}, u32[]{:S(2)}) collective-permute-start(bf16[192,1024]{1,0:T(8,128)(2,1)S(1)} %pad_maximum_fusion), channel_id=1, source_target_pairs={{2,0},{4,2},{6,4},{7,6},{5,7},{3,5},{1,3},{0,1},{10,8},{12,10},{14... | collective-permute-start | bytes 1179656 | tf_op jit(solution)/shard_map/ppermute | solution.py:199
  207.7 10.0 %collective-permute-start.184 = (bf16[192,1024]{1,0:T(8,128)(2,1)S(1)}, bf16[192,1024]{1,0:T(8,128)(2,1)S(1)}, u32[]{:S(2)}, u32[]{:S(2)}) collective-permute-start(bf16[192,1024]{1,0:T(8,128)(2,1)S(1)} %pad_maximum_fusion.1), channel_id=1, source_target_pairs={{0,2},{2,4},{4,6},{6,7},{7,5},{5,3},{3,1},{1,0},{8,10},{10,12},{12... | collective-permute-start | bytes 1179656 | tf_op jit(solution)/shard_map/ppermute | solution.py:200
  217.7 10.8 %collective-permute-start.181 = (bf16[192,1024]{1,0:T(8,128)(2,1)S(1)}, bf16[192,1024]{1,0:T(8,128)(2,1)S(1)}, u32[]{:S(2)}, u32[]{:S(2)}) collective-permute-start(bf16[192,1024]{1,0:T(8,128)(2,1)S(1)} %add_convert_fusion.4), channel_id=1, source_target_pairs={{2,0},{4,2},{6,4},{7,6},{5,7},{3,5},{1,3},{0,1},{10,8},{12,10},{14... | collective-permute-start | bytes 1179656 | tf_op jit(solution)/shard_map/ppermute | solution.py:199
  218.9 10.8 %collective-permute-start.185 = (bf16[192,1024]{1,0:T(8,128)(2,1)S(1)}, bf16[192,1024]{1,0:T(8,128)(2,1)S(1)}, u32[]{:S(2)}, u32[]{:S(2)}) collective-permute-start(bf16[192,1024]{1,0:T(8,128)(2,1)S(1)} %add_convert_fusion.2), channel_id=1, source_target_pairs={{0,2},{2,4},{4,6},{6,7},{7,5},{5,3},{3,1},{1,0},{8,10},{10,12},{12... | collective-permute-start | bytes 1179656 | tf_op jit(solution)/shard_map/ppermute | solution.py:200
  229.6 13.3 %collective-permute-start.182 = (bf16[192,1024]{1,0:T(8,128)(2,1)S(1)}, bf16[192,1024]{1,0:T(8,128)(2,1)S(1)}, u32[]{:S(2)}, u32[]{:S(2)}) collective-permute-start(bf16[192,1024]{1,0:T(8,128)(2,1)S(1)} %add_convert_fusion.3), channel_id=1, source_target_pairs={{2,0},{4,2},{6,4},{7,6},{5,7},{3,5},{1,3},{0,1},{10,8},{12,10},{14... | collective-permute-start | bytes 1179656 | tf_op jit(solution)/shard_map/ppermute | solution.py:199
  230.8 12.1 %collective-permute-start.186 = (bf16[192,1024]{1,0:T(8,128)(2,1)S(1)}, bf16[192,1024]{1,0:T(8,128)(2,1)S(1)}, u32[]{:S(2)}, u32[]{:S(2)}) collective-permute-start(bf16[192,1024]{1,0:T(8,128)(2,1)S(1)} %add_convert_fusion.1), channel_id=1, source_target_pairs={{0,2},{2,4},{4,6},{6,7},{7,5},{5,3},{3,1},{1,0},{8,10},{10,12},{12... | collective-permute-start | bytes 1179656 | tf_op jit(solution)/shard_map/ppermute | solution.py:200
  240.1 2.8 %copy-start.5 = (bf16[192,1024]{1,0:T(8,128)(2,1)S(1)}, bf16[192,1024]{1,0:T(8,128)(2,1)}, u32[]{:S(2)}) copy-start(bf16[192,1024]{1,0:T(8,128)(2,1)} %get-tuple-element.284) | copy-start | bytes 1179652

commit v2 on v1

v2 whole, which is shorter than its diff:
```python
import functools
import itertools

import jax
import jax.numpy as jnp
from jax import lax
from jax.experimental import pallas as pl
from jax.experimental.pallas import tpu as pltpu
from jax.sharding import PartitionSpec as P


LANES = 128
PAIR_LIMIT = 64


def ring_pairs(count, hops):
    order = list(range(0, count, 2)) + list(range(1, count, 2))[::-1]
    ahead = [(order[i], order[(i + hops) % count]) for i in range(count)]
    return ahead, [(b, a) for a, b in ahead]


def relay_of(source, target, count):
    if source ^ 1 != target:
        return source ^ 1
    beyond = target + 2
    return beyond if beyond < count else target - 2


def swap_slots(pair, dp_count, count, weights, moments):
    low, high = pair
    low_relay, high_relay = relay_of(low, high, count), relay_of(high, low, count)

    def spread(core, edges):
        return [
            (row * count + a, row * count + b) for row in range(core, dp_count, 2) for a, b in edges
        ]

    swap = [(low, high), (high, low)]
    first_hop = spread(1, [(low, low_relay), (high, high_relay)])
    second_hop = spread(1, [(low_relay, high), (high_relay, low)])
    axes = ("dp", "expert")
    direct = lax.ppermute(moments, axes, spread(0, swap) + first_hop)
    moved_weights = lax.ppermute(weights, axes, spread(0, swap) + spread(1, swap))
    relayed = lax.ppermute(direct, axes, second_hop)
    return moved_weights, direct, relayed


def any_permutation(source_slot, weights, moments):
    count = lax.axis_size("expert")

    def move(block):
        rows = block.reshape(count, -1, block.shape[-1])
        spread = lax.all_to_all(rows, "expert", split_axis=0, concat_axis=0, tiled=True)
        ordered = jnp.take(spread, source_slot, axis=0)
        back = lax.all_to_all(ordered, "expert", split_axis=0, concat_axis=0, tiled=True)
        return back.reshape(block.shape)

    moved = move(moments)
    return move(weights), moved, moved


def relocate(weights, moments, old_owner, new_owner, source_slot, dp_count, count):
    packed = jnp.concatenate([m.astype(jnp.bfloat16) for m in moments], axis=0)
    pairs = list(itertools.combinations(range(count), 2))
    if len(pairs) > PAIR_LIMIT:
        return any_permutation(source_slot, weights, packed)
    differs = old_owner != new_owner
    low = jnp.min(jnp.where(differs, old_owner, count))
    high = jnp.max(jnp.where(differs, old_owner, 0))
    number = low * count - low * (low + 1) // 2 + high - low - 1
    branch = jnp.where(jnp.sum(differs.astype(jnp.int32)) == 2, number, len(pairs))
    branches = [
        functools.partial(lambda pair, *p: swap_slots(pair, dp_count, count, *p), pair)
        for pair in pairs
    ] + [lambda *p: any_permutation(source_slot, *p)]
    return lax.switch(branch, branches, weights, packed)


def expert_kernel(blocks, shards, width, count, slot_ref, *refs):
    rows_refs, weight_refs, out_refs = (
        refs[:blocks],
        refs[blocks : blocks + shards],
        refs[blocks + shards :],
    )
    rows = jnp.concatenate([r[:, :width] for r in rows_refs], axis=0)
    extra = jnp.concatenate([r[:, width:] for r in rows_refs], axis=0).astype(jnp.float32)
    lane = lax.broadcasted_iota(jnp.int32, extra.shape, 1)
    slot = slot_ref[0]
    mine = (lane == slot) | (lane == slot + count)
    gate = jnp.sum(jnp.where(mine, extra, 0.0), axis=1, keepdims=True)
    total = None
    for w in weight_refs:
        g = jnp.dot(rows, w[0, 0], preferred_element_type=jnp.float32)
        u = jnp.dot(rows, w[0, 1], preferred_element_type=jnp.float32)
        hidden = (g / (1.0 + jnp.exp(-g)) * u).astype(jnp.bfloat16)
        part = lax.dot_general(
            hidden, w[0, 2], (((1,), (1,)), ((), ())), preferred_element_type=jnp.float32
        )
        total = part if total is None else total + part
    result = total.astype(jnp.bfloat16).astype(jnp.float32) * gate
    start = 0
    for out in out_refs:
        out[...] = result[start : start + out.shape[0]].astype(out.dtype)
        start += out.shape[0]


def run_expert(slot, row_blocks, dtype, shards, width, count):
    blocks = len(row_blocks)
    whole = pl.BlockSpec(memory_space=pltpu.VMEM)
    rows = sum(b.shape[0] for b in row_blocks)
    hidden = sum(s.shape[3] for s in shards)
    return pl.pallas_call(
        functools.partial(expert_kernel, blocks, len(shards), width, count),
        out_shape=[jax.ShapeDtypeStruct((b.shape[0], width), dtype) for b in row_blocks],
        in_specs=[pl.BlockSpec(memory_space=pltpu.SMEM)] + [whole] * (blocks + len(shards)),
        out_specs=[whole] * blocks,
        cost_estimate=pl.CostEstimate(
            flops=6 * rows * width * hidden,
            bytes_accessed=6 * width * hidden + 6 * rows * width,
            transcendentals=rows * hidden,
        ),
    )(slot, *row_blocks, *shards)


def whole(
    tokens, route_ids, gate_weight, old_owner, new_owner, weights, first_moment, second_moment
):
    count, dp_count = lax.axis_size("expert"), lax.axis_size("dp")
    tok_rows, width = tokens.shape
    odd = lax.axis_index("dp") % 2 == 1
    labels = jnp.arange(count, dtype=jnp.int32)
    source_slot = jnp.sum(
        jnp.where(new_owner[None, :] == labels[:, None], old_owner[None, :], 0), axis=1
    )
    slot = lax.axis_index("expert").astype(jnp.int32)

    swap = [(i, i ^ 1) for i in range(dp_count)]
    far = []
    for step in range(1, dp_count // 2):
        turn = [(i, (i + 2 * step) % dp_count) for i in range(dp_count)]
        far.append(lax.ppermute(weights, "dp", turn))
    shards = [weights, lax.ppermute(weights, "dp", swap)]

    by_expert = jnp.sum(
        jnp.where(route_ids[:, :, None] == labels[None, None, :], gate_weight[:, :, None], 0.0),
        axis=1,
    )
    by_slot = jnp.sum(
        jnp.where(old_owner[None, None, :] == labels[None, :, None], by_expert[:, None, :], 0.0),
        axis=2,
    )
    high = by_slot.astype(jnp.bfloat16)
    low = (by_slot - high.astype(jnp.float32)).astype(jnp.bfloat16)
    spare = -(-2 * count // LANES) * LANES - 2 * count
    packed = jnp.concatenate([tokens, high, low, jnp.zeros((tok_rows, spare), jnp.bfloat16)], axis=1)

    ahead, behind = ring_pairs(count, 1)
    ahead_two, behind_two = ring_pairs(count, 2)
    opposite = [
        (row * count + a, row * count + b)
        for row in range(dp_count)
        for a, b in (behind if row % 2 else ahead)
    ]
    back_again = [(b, a) for a, b in opposite]
    steps = count // 2
    from_behind = [packed, lax.ppermute(packed, "expert", ahead)]
    from_ahead = [packed, lax.ppermute(packed, "expert", behind)]
    if steps > 2:
        from_behind.append(lax.ppermute(packed, "expert", ahead_two))
        from_ahead.append(lax.ppermute(packed, "expert", behind_two))

    moved = relocate(
        weights,
        (first_moment, second_moment),
        old_owner,
        new_owner,
        source_slot,
        dp_count,
        count,
    )
    moved, far, from_behind[1:], from_ahead[1:] = lax.optimization_barrier(
        (moved, far, from_behind[1:], from_ahead[1:])
    )
    for shard in far:
        shards += [shard, lax.ppermute(shard, "dp", swap)]
    for _ in range(3, steps):
        from_behind.append(lax.ppermute(from_behind[-1], "expert", ahead))
        from_ahead.append(lax.ppermute(from_ahead[-1], "expert", behind))
    farthest = lax.ppermute(
        jnp.where(odd, from_ahead[-1], from_behind[-1]), ("dp", "expert"), opposite
    )

    apply = functools.partial(
        run_expert, slot.reshape(1), shards=shards, width=width, count=count
    )
    own, *near = apply([packed, from_behind[1], from_ahead[1]], jnp.float32)
    answers = {1: near}
    for step in range(2, steps):
        answers[step] = apply([from_behind[step], from_ahead[step]], jnp.float32)
    (outermost,) = apply([farthest], jnp.bfloat16)

    arrived = lax.ppermute(outermost, ("dp", "expert"), back_again).astype(jnp.float32)
    to_behind, to_ahead = jnp.where(odd, 0.0, arrived), jnp.where(odd, arrived, 0.0)
    for step in range(steps - 1, 0, -1):
        back, front = answers[step]
        back = (back + to_behind).astype(jnp.bfloat16)
        front = (front + to_ahead).astype(jnp.bfloat16)
        to_behind = lax.ppermute(back, "expert", behind).astype(jnp.float32)
        to_ahead = lax.ppermute(front, "expert", ahead).astype(jnp.float32)
    layer_output = (own + to_behind + to_ahead).astype(jnp.bfloat16)

    here = jnp.sum(jnp.where(labels == slot, source_slot, 0)) != slot
    moved_weights, direct, relayed = moved
    new_weights = jnp.where(here, moved_weights, weights)
    new_moments = [
        jnp.where(here, jnp.where(odd, relayed[i], direct[i]).astype(m.dtype), m[0])[None]
        for i, m in enumerate((first_moment, second_moment))
    ]
    return (layer_output, new_weights, *new_moments)


def solution(mesh):
    placed = (
        P(("dp", "expert"), None),
        P(("dp", "expert"), None),
        P(("dp", "expert"), None),
        P(),
        P(),
        P("expert", None, None, "dp"),
        P("expert", None, None, "dp"),
        P("expert", None, None, "dp"),
    )
    return jax.shard_map(
        whole,
        mesh=mesh,
        in_specs=placed,
        out_specs=(
            P(("dp", "expert"), None),
            P("expert", None, None, "dp"),
            P("expert", None, None, "dp"),
            P("expert", None, None, "dp"),
        ),
        check_vma=False,
    )
```

time: 242 us -> 241 us (level); the launches traced: 244 us -> 237 us
  starting transfers between devices: 125 us -> 82.3 us
  waiting for transfers between devices: 56.7 us -> 95.4 us
  local copies, waits for them, and re-layouts: 6.42 us -> 3.77 us
    ppermute x25 -> x20, starting transfers between devices: 125 us -> 82.3 us  [the longest x1 13.9 us: whole(): from_ahead = [packed, lax.ppermute(packed, 'expert', behind)]]
    ppermute x25 -> x20, waiting for transfers between devices: 56.7 us -> 95.4 us  [the longest x1 36.7 us: swap_slots(): direct = lax.ppermute(moments, axes, spread(0, swap) + first_hop)]
    select_n x2 -> x3, other arithmetic: 10.2 us -> 10.7 us  [the longest x1 7.6 us: whole(): jnp.where(here, jnp.where(odd, relayed[i], direct[i]).astype(m.dtype), m[0])]
    convert_element_type x10 -> x9, other arithmetic: 9.98 us -> 9.73 us  [the longest x3 4.17 us: whole(): back = (back + to_behind).astype(jnp.bfloat16)]
  transfers between devices with their start and end apart: 25 -> 20, of which waited for: 12 -> 9; matrix products, arithmetic and copies ran while one was open for 11% -> 10% of each run, Pallas kernels for 8% -> 9%
where the time goes in v2:
time: 241 us; the launch traced here: 237 us
  waiting for transfers between devices  95.4 us (40%)
  starting transfers between devices  82.3 us (34%)
  Pallas kernels  26.1 us (11%)
  other arithmetic  24.3 us (10%)
  between operations  5.36 us (2%)
  local copies, waits for them, and re-layouts  3.77 us (2%)
    ppermute x1, waiting for transfers between devices, swap_slots(): direct = lax.ppermute(moments, axes, spread(0, swap) + first_hop)  36.7 us
    pallas_call x4, Pallas kernels, run_expert(): pl.pallas_call(functools.partial(expert_kernel, blocks, len(shards), widt...  26.1 us
    ppermute x1, waiting for transfers between devices, swap_slots(): relayed = lax.ppermute(direct, axes, second_hop)  22.5 us
    ppermute x1, starting transfers between devices, whole(): from_ahead = [packed, lax.ppermute(packed, 'expert', behind)]  13.9 us
    ppermute x1, waiting for transfers between devices, whole(): from_behind.append(lax.ppermute(from_behind[-1], 'expert', ahead))  10.4 us
    ppermute x1, starting transfers between devices, swap_slots(): lax.ppermute(weights, axes, spread(0, swap) + spread(1, swap))  10.4 us
    ppermute x1, waiting for transfers between devices, whole(): from_ahead = [packed, lax.ppermute(packed, 'expert', behind)]  9.9 us
    ppermute x1, starting transfers between devices, whole(): shards += [shard, lax.ppermute(shard, 'dp', swap)]  8.74 us
  transfers between devices with their start and end apart: 20, of which 9 were waited for; matrix products, arithmetic and copies ran while one was open for 10% of the time, Pallas kernels for 9%

profile of v2, /device:TPU:1, one launch (start us, length us, event | category | flops | bytes accessed | tf_op | source)
XLA Modules:
  0.0 237.3 jit_solution(13738919398159352702)
XLA Ops:
  0.6 0.0 copy-start.1
  0.6 7.0 %collective-permute-start.84 = (bf16[1,3,1024,256]{3,2,1,0:T(8,128)(2,1)}, bf16[1,3,1024,256]{3,2,1,0:T(8,128)(2,1)}, u32[]{:S(2)}, u32[]{:S(2)}) collective-permute-start(bf16[1,3,1024,256]{3,2,1,0:T(8,128)(2,1)} %refs_1_.1), channel_id=1, source_target_pairs={{0,16},{8,24},{16,0},{24,8},{1,17},{9,25},{17,1},{25,9},{2,18},{10... | collective-permute-start | bytes 4718600 | tf_op jit(solution)/shard_map/ppermute | solution.py:141
  7.7 0.7 select_reduce_fusion.1
  8.4 0.7 iota_compare_fusion.2
  9.1 0.1 select_reduce_fusion
  9.2 0.1 copy.14
  9.3 0.1 copy.15
  9.5 1.9 concatenate.6.refs_0_
  11.3 1.4 collective-permute-start.85
  12.7 4.9 %collective-permute-start.86 = (bf16[192,1152]{1,0:T(8,128)(2,1)}, bf16[192,1152]{1,0:T(8,128)(2,1)}, u32[]{:S(2)}, u32[]{:S(2)}) collective-permute-start(bf16[192,1152]{1,0:T(8,128)(2,1)} %concatenate.6.refs_0_), channel_id=1, source_target_pairs={{0,4},{2,6},{4,7},{6,5},{7,3},{5,1},{3,0},{1,2},{8,12},{10,14},{12... | collective-permute-start | bytes 1327112 | tf_op jit(solution)/shard_map/ppermute | solution.py:169
  17.6 1.3 select_reduce_fusion.3
  22.9 2.0 convert_element_type.72
  24.9 0.0 copy-start.5
  25.0 0.0 copy-start.6
  25.0 0.2 convert_element_type.73
  25.1 0.5 copy-done.5
  25.6 0.0 copy-done.6
  25.6 0.1 select_reduce_fusion.2
  25.7 0.3 pad_maximum_fusion
  26.0 1.1 copy-done
  27.1 79.9 %conditional.1 = (bf16[1,3,1024,256]{3,2,1,0:T(8,128)(2,1)}, bf16[2,3,1024,256]{3,2,1,0:T(8,128)(2,1)}, bf16[2,3,1024,256]{3,2,1,0:T(8,128)(2,1)}) conditional(s32[]{:T(128)} %clamp.3, (bf16[1,3,1024,256]{3,2,1,0:T(8,128)(2,1)S(1)}, bf16[2,3,1024,256]{3,2,1,0:T(8,128)(2,1)S(1)}) %tuple.180, ...), branch_computations={%region_6.7_spmd, %region_7.8_spmd, %region_8.9_spmd, %region_9.10... | conditional | flops 2360392 | bytes 50336080 | solution.py:76
  27.1 6.4 %collective-permute-start.25 = (bf16[2,3,1024,256]{3,2,1,0:T(8,128)(2,1)S(1)}, bf16[2,3,1024,256]{3,2,1,0:T(8,128)(2,1)}, u32[]{:S(2)}, u32[]{:S(2)}) collective-permute-start(bf16[2,3,1024,256]{3,2,1,0:T(8,128)(2,1)S(1)} %get-tuple-element.135), channel_id=1, source_target_pairs={{1,3},{3,1},{17,19},{19,17},{9,8},{11,10},{25,24},{27,26}} | collective-permute-start | bytes 9437192 | tf_op jit(solution)/shard_map/cond/branch_8_fun/ppermute | solution.py:42
  33.5 36.7 %collective-permute-done.25 = bf16[2,3,1024,256]{3,2,1,0:T(8,128)(2,1)} collective-permute-done((bf16[2,3,1024,256]{3,2,1,0:T(8,128)(2,1)S(1)}, bf16[2,3,1024,256]{3,2,1,0:T(8,128)(2,1)}, u32[]{:S(2)}, u32[]{:S(2)}) %collective-permute-start.25) | collective-permute-done | bytes 3145760 | tf_op jit(solution)/shard_map/cond/branch_8_fun/ppermute | solution.py:42
  70.2 3.9 %collective-permute-start.26 = (bf16[2,3,1024,256]{3,2,1,0:T(8,128)(2,1)}, bf16[2,3,1024,256]{3,2,1,0:T(8,128)(2,1)}, u32[]{:S(2)}, u32[]{:S(2)}) collective-permute-start(bf16[2,3,1024,256]{3,2,1,0:T(8,128)(2,1)} %collective-permute-done.25), channel_id=1, source_target_pairs={{8,11},{10,9},{24,27},{26,25}} | collective-permute-start | bytes 9437192 | tf_op jit(solution)/shard_map/cond/branch_8_fun/ppermute | solution.py:44
  74.2 10.4 %collective-permute-start.24 = (bf16[1,3,1024,256]{3,2,1,0:T(8,128)(2,1)S(1)}, bf16[1,3,1024,256]{3,2,1,0:T(8,128)(2,1)}, u32[]{:S(2)}, u32[]{:S(2)}) collective-permute-start(bf16[1,3,1024,256]{3,2,1,0:T(8,128)(2,1)S(1)} %get-tuple-element.134), channel_id=1, source_target_pairs={{1,3},{3,1},{17,19},{19,17},{9,11},{11,9},{25,27},{27,25}} | collective-permute-start | bytes 4718600 | tf_op jit(solution)/shard_map/cond/branch_8_fun/ppermute | solution.py:43
  84.5 22.5 %collective-permute-done.26 = bf16[2,3,1024,256]{3,2,1,0:T(8,128)(2,1)} collective-permute-done((bf16[2,3,1024,256]{3,2,1,0:T(8,128)(2,1)}, bf16[2,3,1024,256]{3,2,1,0:T(8,128)(2,1)}, u32[]{:S(2)}, u32[]{:S(2)}) %collective-permute-start.26) | collective-permute-done | bytes 3145760 | tf_op jit(solution)/shard_map/cond/branch_8_fun/ppermute | solution.py:44
  107.0 13.9 %collective-permute-start.87 = (bf16[192,1152]{1,0:T(8,128)(2,1)}, bf16[192,1152]{1,0:T(8,128)(2,1)}, u32[]{:S(2)}, u32[]{:S(2)}) collective-permute-start(bf16[192,1152]{1,0:T(8,128)(2,1)} %concatenate.6.refs_0_), channel_id=1, source_target_pairs={{2,0},{4,2},{6,4},{7,6},{5,7},{3,5},{1,3},{0,1},{10,8},{12,10},{14... | collective-permute-start | bytes 1327112 | tf_op jit(solution)/shard_map/ppermute | solution.py:167
  120.9 2.7 %collective-permute-start.88 = (bf16[192,1152]{1,0:T(8,128)(2,1)}, bf16[192,1152]{1,0:T(8,128)(2,1)}, u32[]{:S(2)}, u32[]{:S(2)}) collective-permute-start(bf16[192,1152]{1,0:T(8,128)(2,1)} %concatenate.6.refs_0_), channel_id=1, source_target_pairs={{4,0},{6,2},{7,4},{5,6},{3,7},{1,5},{0,3},{2,1},{12,8},{14,10},{15... | collective-permute-start | bytes 1327112 | tf_op jit(solution)/shard_map/ppermute | solution.py:170
  123.7 0.0 collective-permute-done.85.refs_1_
  123.7 5.7 %collective-permute-start.89 = (bf16[1,3,1024,256]{3,2,1,0:T(8,128)(2,1)S(1)}, bf16[1,3,1024,256]{3,2,1,0:T(8,128)(2,1)S(1)}, u32[]{:S(2)}, u32[]{:S(2)}) collective-permute-start(bf16[1,3,1024,256]{3,2,1,0:T(8,128)(2,1)S(1)} %copy-done), channel_id=1, source_target_pairs={{0,8},{8,0},{16,24},{24,16},{1,9},{9,1},{17,25},{25,17},{2,10},{10... | collective-permute-start | bytes 4718600 | tf_op jit(solution)/shard_map/ppermute | solution.py:142
  129.4 0.0 collective-permute-done.86.refs_0_
  129.4 9.9 %collective-permute-done.87.refs_2_ = bf16[192,1152]{1,0:T(8,128)(2,1)} collective-permute-done((bf16[192,1152]{1,0:T(8,128)(2,1)}, bf16[192,1152]{1,0:T(8,128)(2,1)}, u32[]{:S(2)}, u32[]{:S(2)}) %collective-permute-start.87) | collective-permute-done | bytes 442400 | tf_op jit(solution)/shard_map/ppermute | solution.py:167
  139.3 6.6 %collective-permute-done.88.refs_1_ = bf16[192,1152]{1,0:T(8,128)(2,1)} collective-permute-done((bf16[192,1152]{1,0:T(8,128)(2,1)}, bf16[192,1152]{1,0:T(8,128)(2,1)}, u32[]{:S(2)}, u32[]{:S(2)}) %collective-permute-start.88) | collective-permute-done | bytes 442400 | tf_op jit(solution)/shard_map/ppermute | solution.py:170
  145.9 0.0 collective-permute-done.84.refs_5_.refs_4_.refs_3_
  145.9 8.7 %collective-permute-start.90 = (bf16[1,3,1024,256]{3,2,1,0:T(8,128)(2,1)}, bf16[1,3,1024,256]{3,2,1,0:T(8,128)(2,1)}, u32[]{:S(2)}, u32[]{:S(2)}) collective-permute-start(bf16[1,3,1024,256]{3,2,1,0:T(8,128)(2,1)} %collective-permute-done.84.refs_5_.refs_4_.refs_3_), channel_id=1, source_target_pairs={{0,8},{8,0},{16,24},{24,16},{1,9},{9,1},{17,25},{25,17},{2,10},{10... | collective-permute-start | bytes 4718600 | tf_op jit(solution)/shard_map/ppermute | solution.py:185
  154.6 1.4 collective-permute-start.91
  156.0 0.1 collective-permute-start.92
  156.1 10.4 %collective-permute-done.91.refs_0_ = bf16[192,1152]{1,0:T(8,128)(2,1)} collective-permute-done((bf16[192,1152]{1,0:T(8,128)(2,1)}, bf16[192,1152]{1,0:T(8,128)(2,1)}, u32[]{:S(2)}, u32[]{:S(2)}) %collective-permute-start.91) | collective-permute-done | bytes 442400 | tf_op jit(solution)/shard_map/ppermute | solution.py:187
  166.5 0.9 collective-permute-done.92.refs_1_
  167.3 1.8 broadcast_select_fusion.3
  169.2 5.8 %collective-permute-start.93 = (bf16[192,1152]{1,0:T(8,128)(2,1)}, bf16[192,1152]{1,0:T(8,128)(2,1)}, u32[]{:S(2)}, u32[]{:S(2)}) collective-permute-start(bf16[192,1152]{1,0:T(8,128)(2,1)} %broadcast_select_fusion.3), channel_id=1, source_target_pairs={{0,2},{2,4},{4,6},{6,7},{7,5},{5,3},{3,1},{1,0},{10,8},{12,10},{14... | collective-permute-start | bytes 1327112 | tf_op jit(solution)/shard_map/ppermute | solution.py:189
  175.0 7.6 %collective-permute-done.93.refs_0_ = bf16[192,1152]{1,0:T(8,128)(2,1)} collective-permute-done((bf16[192,1152]{1,0:T(8,128)(2,1)}, bf16[192,1152]{1,0:T(8,128)(2,1)}, u32[]{:S(2)}, u32[]{:S(2)}) %collective-permute-start.93) | collective-permute-done | bytes 442400 | tf_op jit(solution)/shard_map/ppermute | solution.py:189
  182.6 5.1 %shard_map.114 = bf16[192,1024]{1,0:T(8,128)(2,1)} custom-call(s32[1]{0:T(128)} %bitcast.4.slot_ref, bf16[192,1152]{1,0:T(8,128)(2,1)} %collective-permute-done.93.refs_0_, bf16[1,3,1024,256]{3,2,1,0:T(8,128)(2,1)S(1)} %copy-done, bf16[1,3,1024,256]{3,2,1,0:T(8,128)(2,1)} %copy-done.3, ...), custom_call_target="tpu_custom_call" | custom-call | flops 1207959552 | bytes 7471104 | tf_op jit(solution)/shard_map/pallas_call | solution.py:112
  187.7 5.2 %collective-permute-start.94 = (bf16[192,1024]{1,0:T(8,128)(2,1)}, bf16[192,1024]{1,0:T(8,128)(2,1)S(1)}, u32[]{:S(2)}, u32[]{:S(2)}) collective-permute-start(bf16[192,1024]{1,0:T(8,128)(2,1)} %shard_map.114), channel_id=1, source_target_pairs={{2,0},{4,2},{6,4},{7,6},{5,7},{3,5},{1,3},{0,1},{8,10},{10,12},{12... | collective-permute-start | bytes 1179656 | tf_op jit(solution)/shard_map/ppermute | solution.py:202
  193.0 6.5 %shard_map.113 = (f32[192,1024]{1,0:T(8,128)}, f32[192,1024]{1,0:T(8,128)}) custom-call(s32[1]{0:T(128)} %bitcast.4.slot_ref, bf16[192,1152]{1,0:T(8,128)(2,1)} %collective-permute-done.91.refs_0_, bf16[192,1152]{1,0:T(8,128)(2,1)} %collective-permute-done.92.refs_1_, bf16[1,3,1024,256]{3,2,1,0:T(8,128)(2,1)S(1)} %copy-done, ...), custom_call_target="tpu_custom_call" | custom-call | flops 2415919104 | bytes 8650752 | tf_op jit(solution)/shard_map/pallas_call | solution.py:112
  199.5 0.5 collective-permute-done.94
  200.0 1.6 fusion.1
  201.6 0.9 collective-permute-start.95
  202.5 0.6 fusion.4
  203.8 0.6 collective-permute-start.98
  204.4 6.5 %shard_map.112 = (f32[192,1024]{1,0:T(8,128)}, f32[192,1024]{1,0:T(8,128)}) custom-call(s32[1]{0:T(128)} %bitcast.4.slot_ref, bf16[192,1152]{1,0:T(8,128)(2,1)} %collective-permute-done.86.refs_0_, bf16[192,1152]{1,0:T(8,128)(2,1)} %collective-permute-done.88.refs_1_, bf16[1,3,1024,256]{3,2,1,0:T(8,128)(2,1)S(1)} %copy-done, ...), custom_call_target="tpu_custom_call" | custom-call | flops 2415919104 | bytes 8650752 | tf_op jit(solution)/shard_map/pallas_call | solution.py:112
  211.0 0.4 collective-permute-done.95
  211.3 1.2 add_convert_fusion.4
  212.6 1.5 collective-permute-start.96
  214.1 1.2 add_convert_fusion.2
  215.3 0.1 collective-permute-start.99
  215.4 7.9 %shard_map.111 = (f32[192,1024]{1,0:T(8,128)}, f32[192,1024]{1,0:T(8,128)}, f32[192,1024]{1,0:T(8,128)}) custom-call(s32[1]{0:T(128)} %bitcast.4.slot_ref, bf16[192,1152]{1,0:T(8,128)(2,1)} %concatenate.6.refs_0_, bf16[192,1152]{1,0:T(8,128)(2,1)} %collective-permute-done.85.refs_1_, bf16[192,1152]{1,0:T(8,128)(2,1)} %collective-permute-done.87.refs_2_, ...), custom_call_target="tpu_custom_call" | custom-call | flops 3623878656 | bytes 9830400 | tf_op jit(solution)/shard_map/pallas_call | solution.py:112
  223.3 1.4 add_convert_fusion.3
  224.7 1.5 collective-permute-start.97
  226.2 1.2 add_convert_fusion.1
  227.4 0.1 collective-permute-start.100
  227.5 7.6 %convert_select_fusion = (f32[1,3,1024,256]{3,2,1,0:T(8,128)}, f32[1,3,1024,256]{3,2,1,0:T(8,128)}) fusion(f32[1,3,1024,256]{3,2,1,0:T(8,128)S(1)} %copy-done.2, bf16[2,3,1024,256]{3,2,1,0:T(8,128)(2,1)} %get-tuple-element.216, bf16[2,3,1024,256]{3,2,1,0:T(8,128)(2,1)} %get-tuple-element.215, pred[]{:T(512)S(6)} %eq.68, pred[]{:T(512)S(6)} %ne.24, ...), kind=kLoop, calls=%fused_computation.8 | loop fusion | flops 4718592 | bytes 18874370 | tf_op jit(solution)/shard_map/jit(_where)/select_n | solution.py:216
  235.1 1.3 broadcast_select_fusion.2
  236.4 0.9 add_convert_fusion
  (18 shorter events, 0.1 us)
Async XLA Ops:
  0.6 24.3 %copy-start.1 = (f32[1,3,1024,256]{3,2,1,0:T(8,128)S(1)}, f32[1,3,1024,256]{3,2,1,0:T(8,128)}, u32[]{:S(2)}) copy-start(f32[1,3,1024,256]{3,2,1,0:T(8,128)} %param.44) | copy-start | bytes 9437188
  0.6 145.2 %collective-permute-start.84 = (bf16[1,3,1024,256]{3,2,1,0:T(8,128)(2,1)}, bf16[1,3,1024,256]{3,2,1,0:T(8,128)(2,1)}, u32[]{:S(2)}, u32[]{:S(2)}) collective-permute-start(bf16[1,3,1024,256]{3,2,1,0:T(8,128)(2,1)} %refs_1_.1), channel_id=1, source_target_pairs={{0,16},{8,24},{16,0},{24,8},{1,17},{9,25},{17,1},{25,9},{2,18},{10... | collective-permute-start | bytes 4718600 | tf_op jit(solution)/shard_map/ppermute | solution.py:141
  11.3 112.3 %collective-permute-start.85 = (bf16[192,1152]{1,0:T(8,128)(2,1)}, bf16[192,1152]{1,0:T(8,128)(2,1)}, u32[]{:S(2)}, u32[]{:S(2)}) collective-permute-start(bf16[192,1152]{1,0:T(8,128)(2,1)} %concatenate.6.refs_0_), channel_id=1, source_target_pairs={{0,2},{2,4},{4,6},{6,7},{7,5},{5,3},{3,1},{1,0},{8,10},{10,12},{12... | collective-permute-start | bytes 1327112 | tf_op jit(solution)/shard_map/ppermute | solution.py:166
  12.7 116.7 %collective-permute-start.86 = (bf16[192,1152]{1,0:T(8,128)(2,1)}, bf16[192,1152]{1,0:T(8,128)(2,1)}, u32[]{:S(2)}, u32[]{:S(2)}) collective-permute-start(bf16[192,1152]{1,0:T(8,128)(2,1)} %concatenate.6.refs_0_), channel_id=1, source_target_pairs={{0,4},{2,6},{4,7},{6,5},{7,3},{5,1},{3,0},{1,2},{8,12},{10,14},{12... | collective-permute-start | bytes 1327112 | tf_op jit(solution)/shard_map/ppermute | solution.py:169
  24.9 0.7 copy-start.5
  25.0 0.7 copy-start.6
  25.7 1.4 copy-start
  27.1 43.1 %collective-permute-start.25 = (bf16[2,3,1024,256]{3,2,1,0:T(8,128)(2,1)S(1)}, bf16[2,3,1024,256]{3,2,1,0:T(8,128)(2,1)}, u32[]{:S(2)}, u32[]{:S(2)}) collective-permute-start(bf16[2,3,1024,256]{3,2,1,0:T(8,128)(2,1)S(1)} %get-tuple-element.135), channel_id=1, source_target_pairs={{1,3},{3,1},{17,19},{19,17},{9,8},{11,10},{25,24},{27,26}} | collective-permute-start | bytes 9437192 | tf_op jit(solution)/shard_map/cond/branch_8_fun/ppermute | solution.py:42
  70.2 36.8 %collective-permute-start.26 = (bf16[2,3,1024,256]{3,2,1,0:T(8,128)(2,1)}, bf16[2,3,1024,256]{3,2,1,0:T(8,128)(2,1)}, u32[]{:S(2)}, u32[]{:S(2)}) collective-permute-start(bf16[2,3,1024,256]{3,2,1,0:T(8,128)(2,1)} %collective-permute-done.25), channel_id=1, source_target_pairs={{8,11},{10,9},{24,27},{26,25}} | collective-permute-start | bytes 9437192 | tf_op jit(solution)/shard_map/cond/branch_8_fun/ppermute | solution.py:44
  74.2 10.4 %collective-permute-start.24 = (bf16[1,3,1024,256]{3,2,1,0:T(8,128)(2,1)S(1)}, bf16[1,3,1024,256]{3,2,1,0:T(8,128)(2,1)}, u32[]{:S(2)}, u32[]{:S(2)}) collective-permute-start(bf16[1,3,1024,256]{3,2,1,0:T(8,128)(2,1)S(1)} %get-tuple-element.134), channel_id=1, source_target_pairs={{1,3},{3,1},{17,19},{19,17},{9,11},{11,9},{25,27},{27,25}} | collective-permute-start | bytes 4718600 | tf_op jit(solution)/shard_map/cond/branch_8_fun/ppermute | solution.py:43
  107.0 32.3 %collective-permute-start.87 = (bf16[192,1152]{1,0:T(8,128)(2,1)}, bf16[192,1152]{1,0:T(8,128)(2,1)}, u32[]{:S(2)}, u32[]{:S(2)}) collective-permute-start(bf16[192,1152]{1,0:T(8,128)(2,1)} %concatenate.6.refs_0_), channel_id=1, source_target_pairs={{2,0},{4,2},{6,4},{7,6},{5,7},{3,5},{1,3},{0,1},{10,8},{12,10},{14... | collective-permute-start | bytes 1327112 | tf_op jit(solution)/shard_map/ppermute | solution.py:167
  120.9 24.9 %collective-permute-start.88 = (bf16[192,1152]{1,0:T(8,128)(2,1)}, bf16[192,1152]{1,0:T(8,128)(2,1)}, u32[]{:S(2)}, u32[]{:S(2)}) collective-permute-start(bf16[192,1152]{1,0:T(8,128)(2,1)} %concatenate.6.refs_0_), channel_id=1, source_target_pairs={{4,0},{6,2},{7,4},{5,6},{3,7},{1,5},{0,3},{2,1},{12,8},{14,10},{15... | collective-permute-start | bytes 1327112 | tf_op jit(solution)/shard_map/ppermute | solution.py:170
  123.7 51.3 %collective-permute-start.89 = (bf16[1,3,1024,256]{3,2,1,0:T(8,128)(2,1)S(1)}, bf16[1,3,1024,256]{3,2,1,0:T(8,128)(2,1)S(1)}, u32[]{:S(2)}, u32[]{:S(2)}) collective-permute-start(bf16[1,3,1024,256]{3,2,1,0:T(8,128)(2,1)S(1)} %copy-done), channel_id=1, source_target_pairs={{0,8},{8,0},{16,24},{24,16},{1,9},{9,1},{17,25},{25,17},{2,10},{10... | collective-permute-start | bytes 4718600 | tf_op jit(solution)/shard_map/ppermute | solution.py:142
  145.9 36.7 %collective-permute-start.90 = (bf16[1,3,1024,256]{3,2,1,0:T(8,128)(2,1)}, bf16[1,3,1024,256]{3,2,1,0:T(8,128)(2,1)}, u32[]{:S(2)}, u32[]{:S(2)}) collective-permute-start(bf16[1,3,1024,256]{3,2,1,0:T(8,128)(2,1)} %collective-permute-done.84.refs_5_.refs_4_.refs_3_), channel_id=1, source_target_pairs={{0,8},{8,0},{16,24},{24,16},{1,9},{9,1},{17,25},{25,17},{2,10},{10... | collective-permute-start | bytes 4718600 | tf_op jit(solution)/shard_map/ppermute | solution.py:185
  154.6 11.9 %collective-permute-start.91 = (bf16[192,1152]{1,0:T(8,128)(2,1)}, bf16[192,1152]{1,0:T(8,128)(2,1)}, u32[]{:S(2)}, u32[]{:S(2)}) collective-permute-start(bf16[192,1152]{1,0:T(8,128)(2,1)} %collective-permute-done.86.refs_0_), channel_id=1, source_target_pairs={{0,2},{2,4},{4,6},{6,7},{7,5},{5,3},{3,1},{1,0},{8,10},{10,12},{12... | collective-permute-start | bytes 1327112 | tf_op jit(solution)/shard_map/ppermute | solution.py:187
  156.0 11.4 %collective-permute-start.92 = (bf16[192,1152]{1,0:T(8,128)(2,1)}, bf16[192,1152]{1,0:T(8,128)(2,1)}, u32[]{:S(2)}, u32[]{:S(2)}) collective-permute-start(bf16[192,1152]{1,0:T(8,128)(2,1)} %collective-permute-done.88.refs_1_), channel_id=1, source_target_pairs={{2,0},{4,2},{6,4},{7,6},{5,7},{3,5},{1,3},{0,1},{10,8},{12,10},{14... | collective-permute-start | bytes 1327112 | tf_op jit(solution)/shard_map/ppermute | solution.py:188
  169.2 13.5 %collective-permute-start.93 = (bf16[192,1152]{1,0:T(8,128)(2,1)}, bf16[192,1152]{1,0:T(8,128)(2,1)}, u32[]{:S(2)}, u32[]{:S(2)}) collective-permute-start(bf16[192,1152]{1,0:T(8,128)(2,1)} %broadcast_select_fusion.3), channel_id=1, source_target_pairs={{0,2},{2,4},{4,6},{6,7},{7,5},{5,3},{3,1},{1,0},{10,8},{12,10},{14... | collective-permute-start | bytes 1327112 | tf_op jit(solution)/shard_map/ppermute | solution.py:189
  175.0 7.7 %copy-start.3 = (bf16[1,3,1024,256]{3,2,1,0:T(8,128)(2,1)}, bf16[1,3,1024,256]{3,2,1,0:T(8,128)(2,1)S(1)}, u32[]{:S(2)}) copy-start(bf16[1,3,1024,256]{3,2,1,0:T(8,128)(2,1)S(1)} %collective-permute-done.89.refs_4_.refs_3_.refs_2_) | copy-start | bytes 4718596
  187.7 12.2 %collective-permute-start.94 = (bf16[192,1024]{1,0:T(8,128)(2,1)}, bf16[192,1024]{1,0:T(8,128)(2,1)S(1)}, u32[]{:S(2)}, u32[]{:S(2)}) collective-permute-start(bf16[192,1024]{1,0:T(8,128)(2,1)} %shard_map.114), channel_id=1, source_target_pairs={{2,0},{4,2},{6,4},{7,6},{5,7},{3,5},{1,3},{0,1},{8,10},{10,12},{12... | collective-permute-start | bytes 1179656 | tf_op jit(solution)/shard_map/ppermute | solution.py:202
  201.6 9.8 %collective-permute-start.95 = (bf16[192,1024]{1,0:T(8,128)(2,1)S(1)}, bf16[192,1024]{1,0:T(8,128)(2,1)S(1)}, u32[]{:S(2)}, u32[]{:S(2)}) collective-permute-start(bf16[192,1024]{1,0:T(8,128)(2,1)S(1)} %get-tuple-element.224), channel_id=1, source_target_pairs={{2,0},{4,2},{6,4},{7,6},{5,7},{3,5},{1,3},{0,1},{10,8},{12,10},{14... | collective-permute-start | bytes 1179656 | tf_op jit(solution)/shard_map/ppermute | solution.py:208
  203.8 10.3 %collective-permute-start.98 = (bf16[192,1024]{1,0:T(8,128)(2,1)S(1)}, bf16[192,1024]{1,0:T(8,128)(2,1)S(1)}, u32[]{:S(2)}, u32[]{:S(2)}) collective-permute-start(bf16[192,1024]{1,0:T(8,128)(2,1)S(1)} %get-tuple-element.225), channel_id=1, source_target_pairs={{0,2},{2,4},{4,6},{6,7},{7,5},{5,3},{3,1},{1,0},{8,10},{10,12},{12... | collective-permute-start | bytes 1179656 | tf_op jit(solution)/shard_map/ppermute | solution.py:209
  212.6 10.7 %collective-permute-start.96 = (bf16[192,1024]{1,0:T(8,128)(2,1)S(1)}, bf16[192,1024]{1,0:T(8,128)(2,1)S(1)}, u32[]{:S(2)}, u32[]{:S(2)}) collective-permute-start(bf16[192,1024]{1,0:T(8,128)(2,1)S(1)} %add_convert_fusion.4), channel_id=1, source_target_pairs={{2,0},{4,2},{6,4},{7,6},{5,7},{3,5},{1,3},{0,1},{10,8},{12,10},{14... | collective-permute-start | bytes 1179656 | tf_op jit(solution)/shard_map/ppermute | solution.py:208
  215.3 10.9 %collective-permute-start.99 = (bf16[192,1024]{1,0:T(8,128)(2,1)S(1)}, bf16[192,1024]{1,0:T(8,128)(2,1)S(1)}, u32[]{:S(2)}, u32[]{:S(2)}) collective-permute-start(bf16[192,1024]{1,0:T(8,128)(2,1)S(1)} %add_convert_fusion.2), channel_id=1, source_target_pairs={{0,2},{2,4},{4,6},{6,7},{7,5},{5,3},{3,1},{1,0},{8,10},{10,12},{12... | collective-permute-start | bytes 1179656 | tf_op jit(solution)/shard_map/ppermute | solution.py:209
  223.3 4.2 %copy-start.2 = (f32[1,3,1024,256]{3,2,1,0:T(8,128)S(1)}, f32[1,3,1024,256]{3,2,1,0:T(8,128)}, u32[]{:S(2)}) copy-start(f32[1,3,1024,256]{3,2,1,0:T(8,128)} %param.44) | copy-start | bytes 9437188
  224.7 11.7 %collective-permute-start.97 = (bf16[192,1024]{1,0:T(8,128)(2,1)S(1)}, bf16[192,1024]{1,0:T(8,128)(2,1)S(1)}, u32[]{:S(2)}, u32[]{:S(2)}) collective-permute-start(bf16[192,1024]{1,0:T(8,128)(2,1)S(1)} %add_convert_fusion.3), channel_id=1, source_target_pairs={{2,0},{4,2},{6,4},{7,6},{5,7},{3,5},{1,3},{0,1},{10,8},{12,10},{14... | collective-permute-start | bytes 1179656 | tf_op jit(solution)/shard_map/ppermute | solution.py:208
  227.4 9.0 %collective-permute-start.100 = (bf16[192,1024]{1,0:T(8,128)(2,1)S(1)}, bf16[192,1024]{1,0:T(8,128)(2,1)S(1)}, u32[]{:S(2)}, u32[]{:S(2)}) collective-permute-start(bf16[192,1024]{1,0:T(8,128)(2,1)S(1)} %add_convert_fusion.1), channel_id=1, source_target_pairs={{0,2},{2,4},{4,6},{6,7},{7,5},{5,3},{3,1},{1,0},{8,10},{10,12},{12... | collective-permute-start | bytes 1179656 | tf_op jit(solution)/shard_map/ppermute | solution.py:209
  235.1 1.3 copy-start.4

commit v3 on v2

--- a/solution.py
+++ b/solution.py
@@ -13,9 +13,9 @@
 PAIR_LIMIT = 64
 
 
-def ring_pairs(count, hops):
+def ring_pairs(count):
     order = list(range(0, count, 2)) + list(range(1, count, 2))[::-1]
-    ahead = [(order[i], order[(i + hops) % count]) for i in range(count)]
+    ahead = [(order[i], order[(i + 1) % count]) for i in range(count)]
     return ahead, [(b, a) for a, b in ahead]
 
 
@@ -59,21 +59,43 @@
     return move(weights), moved, moved
 
 
-def relocate(weights, moments, old_owner, new_owner, source_slot, dp_count, count):
-    packed = jnp.concatenate([m.astype(jnp.bfloat16) for m in moments], axis=0)
+def pack_kernel(first_ref, second_ref, out_ref):
+    out_ref[0] = first_ref[0].astype(jnp.bfloat16)
+    out_ref[1] = second_ref[0].astype(jnp.bfloat16)
+
+
+def pack_moments(first_moment, second_moment):
+    _, parts, rows, lanes = first_moment.shape
+    block = (1, 1, rows, lanes)
+    return pl.pallas_call(
+        pack_kernel,
+        grid=(parts,),
+        out_shape=jax.ShapeDtypeStruct((2, parts, rows, lanes), jnp.bfloat16),
+        in_specs=[pl.BlockSpec(block, lambda i: (0, i, 0, 0))] * 2,
+        out_specs=pl.BlockSpec((2, 1, rows, lanes), lambda i: (0, i, 0, 0)),
+        cost_estimate=pl.CostEstimate(
+            flops=first_moment.size, bytes_accessed=12 * first_moment.size, transcendentals=0
+        ),
+    )(first_moment, second_moment)
+
+
+def relocate(weights, packed, ring, finish, old_owner, new_owner, source_slot, dp_count, count):
     pairs = list(itertools.combinations(range(count), 2))
     if len(pairs) > PAIR_LIMIT:
-        return any_permutation(source_slot, weights, packed)
+        return any_permutation(source_slot, weights, packed), finish(*ring)
     differs = old_owner != new_owner
     low = jnp.min(jnp.where(differs, old_owner, count))
     high = jnp.max(jnp.where(differs, old_owner, 0))
     number = low * count - low * (low + 1) // 2 + high - low - 1
     branch = jnp.where(jnp.sum(differs.astype(jnp.int32)) == 2, number, len(pairs))
-    branches = [
-        functools.partial(lambda pair, *p: swap_slots(pair, dp_count, count, *p), pair)
-        for pair in pairs
-    ] + [lambda *p: any_permutation(source_slot, *p)]
-    return lax.switch(branch, branches, weights, packed)
+
+    def moving(pair, weights, packed, ring):
+        return swap_slots(pair, dp_count, count, weights, packed), finish(*ring)
+
+    branches = [functools.partial(moving, pair) for pair in pairs] + [
+        lambda weights, packed, ring: (any_permutation(source_slot, weights, packed), finish(*ring))
+    ]
+    return lax.switch(branch, branches, weights, packed, ring)
 
 
 def expert_kernel(blocks, shards, width, count, slot_ref, *refs):
@@ -139,8 +161,6 @@
     for step in range(1, dp_count // 2):
         turn = [(i, (i + 2 * step) % dp_count) for i in range(dp_count)]
         far.append(lax.ppermute(weights, "dp", turn))
-    shards = [weights, lax.ppermute(weights, "dp", swap)]
-
     by_expert = jnp.sum(
         jnp.where(route_ids[:, :, None] == labels[None, None, :], gate_weight[:, :, None], 0.0),
         axis=1,
@@ -154,53 +174,61 @@
     spare = -(-2 * count // LANES) * LANES - 2 * count
     packed = jnp.concatenate([tokens, high, low, jnp.zeros((tok_rows, spare), jnp.bfloat16)], axis=1)
 
-    ahead, behind = ring_pairs(count, 1)
-    ahead_two, behind_two = ring_pairs(count, 2)
+    ahead, behind = ring_pairs(count)
     opposite = [
         (row * count + a, row * count + b)
         for row in range(dp_count)
         for a, b in (behind if row % 2 else ahead)
     ]
-    back_again = [(b, a) for a, b in opposite]
     steps = count // 2
-    from_behind = [packed, lax.ppermute(packed, "expert", ahead)]
-    from_ahead = [packed, lax.ppermute(packed, "expert", behind)]
-    if steps > 2:
-        from_behind.append(lax.ppermute(packed, "expert", ahead_two))
-        from_ahead.append(lax.ppermute(packed, "expert", behind_two))
-
-    moved = relocate(
+    from_behind, from_ahead = [packed], [packed]
+    for _ in range(1, min(3, steps)):
+        from_behind.append(lax.ppermute(from_behind[-1], "expert", ahead))
+        from_ahead.append(lax.ppermute(from_ahead[-1], "expert", behind))
+
+    def finish(back, front):
+        backs, fronts = [], []
+        for _ in range(3, steps):
+            back = lax.ppermute(back, "expert", ahead)
+            front = lax.ppermute(front, "expert", behind)
+            backs.append(back)
+            fronts.append(front)
+        outer = lax.ppermute(jnp.where(odd, front, back), ("dp", "expert"), opposite)
+        return backs, fronts, outer
+
+    moments = pack_moments(first_moment, second_moment)
+    moved, (backs, fronts, farthest) = relocate(
         weights,
-        (first_moment, second_moment),
+        moments,
+        (from_behind[-1], from_ahead[-1]),
+        finish,
         old_owner,
         new_owner,
         source_slot,
         dp_count,
         count,
     )
-    moved, far, from_behind[1:], from_ahead[1:] = lax.optimization_barrier(
-        (moved, far, from_behind[1:], from_ahead[1:])
-    )
+    from_behind += backs
+    from_ahead += fronts
+    far, moved = lax.optimization_barrier((far, moved))
+    near = lax.ppermute(weights, "dp", swap)
+    shards = [weights, near]
     for shard in far:
-        shards += [shard, lax.ppermute(shard, "dp", swap)]
-    for _ in range(3, steps):
-        from_behind.append(lax.ppermute(from_behind[-1], "expert", ahead))
-        from_ahead.append(lax.ppermute(from_ahead[-1], "expert", behind))
-    farthest = lax.ppermute(
-        jnp.where(odd, from_ahead[-1], from_behind[-1]), ("dp", "expert"), opposite
-    )
+        shard, near = lax.optimization_barrier((shard, near))
+        near = lax.ppermute(shard, "dp", swap)
+        shards += [shard, near]
 
     apply = functools.partial(
         run_expert, slot.reshape(1), shards=shards, width=width, count=count
     )
-    own, *near = apply([packed, from_behind[1], from_ahead[1]], jnp.float32)
-    answers = {1: near}
-    for step in range(2, steps):
+    (outermost,) = apply([farthest], jnp.bfloat16)
+    answers = {}
+    for step in range(steps - 1, 1, -1):
         answers[step] = apply([from_behind[step], from_ahead[step]], jnp.float32)
-    (outermost,) = apply([farthest], jnp.bfloat16)
-
-    arrived = lax.ppermute(outermost, ("dp", "expert"), back_again).astype(jnp.float32)
-    to_behind, to_ahead = jnp.where(odd, 0.0, arrived), jnp.where(odd, arrived, 0.0)
+    own, *answers[1] = apply([packed, from_behind[1], from_ahead[1]], jnp.float32)
+
+    arrived = lax.ppermute(outermost, ("dp", "expert"), opposite).astype(jnp.float32)
+    to_behind, to_ahead = jnp.where(odd, arrived, 0.0), jnp.where(odd, 0.0, arrived)
     for step in range(steps - 1, 0, -1):
         back, front = answers[step]
         back = (back + to_behind).astype(jnp.bfloat16)

time: 241 us -> 202 us (0.84)
  starting transfers between devices: 82.3 us -> 42.7 us
  Pallas kernels: 26.1 us -> 31.4 us
  other arithmetic: 24.3 us -> 21 us
    ppermute x8 -> x6, starting transfers between devices: 48.4 us -> 12.7 us  [the longest x1 6.69 us: finish(): lax.ppermute(jnp.where(odd, front, back), ('dp', 'expert'), opposite)]
    ppermute x8 -> x6, waiting for transfers between devices: 24.6 us -> 49.5 us  [the longest x1 37.1 us: finish(): back = lax.ppermute(back, 'expert', ahead)]
    ppermute x1, waiting for transfers between devices: 22.5 us -> 0.01 us  [swap_slots(): relayed = lax.ppermute(direct, axes, second_hop)]
    ppermute x1, starting transfers between devices: 10.4 us -> 3.71 us  [swap_slots(): lax.ppermute(weights, axes, spread(0, swap) + spread(1, swap))]
    pallas_call x0 -> x1, Pallas kernels: none -> 5.28 us  [pack_moments(): pl.pallas_call(pack_kernel, grid=(parts,), out_shape=jax.ShapeDtypeStruct...]
    ppermute x3, starting transfers between devices: 3.97 us -> 0.76 us  [whole(): to_behind = lax.ppermute(back, 'expert', behind).astype(jnp.float32)]
    ppermute x3, starting transfers between devices: 0.76 us -> 3.93 us  [whole(): to_ahead = lax.ppermute(front, 'expert', ahead).astype(jnp.float32)]
    ppermute x1 -> x2, waiting for transfers between devices: 10.4 us -> 9.81 us  [whole(): from_behind.append(lax.ppermute(from_behind[-1], 'expert', ahead))]
  transfers between devices with their start and end apart: 20 -> 20, of which waited for: 9 -> 8; matrix products, arithmetic and copies ran while one was open for 10% -> 9% of each run, Pallas kernels for 9% -> 13%
where the time goes in v3:
time: 202 us; the launch traced here: 200 us
  waiting for transfers between devices  97.6 us (48%)
  starting transfers between devices  42.7 us (21%)
  Pallas kernels  31.4 us (16%)
  other arithmetic  21 us (10%)
  between operations  5.4 us (3%)
    ppermute x1, waiting for transfers between devices, finish(): back = lax.ppermute(back, 'expert', ahead)  37.1 us
    ppermute x1, waiting for transfers between devices, swap_slots(): direct = lax.ppermute(moments, axes, spread(0, swap) + first_hop)  36.9 us
    pallas_call x4, Pallas kernels, run_expert(): pl.pallas_call(functools.partial(expert_kernel, blocks, len(shards), widt...  26.1 us
    ppermute x2, waiting for transfers between devices, whole(): from_behind.append(lax.ppermute(from_behind[-1], 'expert', ahead))  9.81 us
    select_n x1, other arithmetic, whole(): jnp.where(here, jnp.where(odd, relayed[i], direct[i]).astype(m.dtype), m[0])  7.53 us
    ppermute x1, starting transfers between devices, whole(): far.append(lax.ppermute(weights, 'dp', turn))  7.52 us
    ppermute x1, starting transfers between devices, finish(): lax.ppermute(jnp.where(odd, front, back), ('dp', 'expert'), opposite)  6.69 us
    ppermute x1, starting transfers between devices, swap_slots(): direct = lax.ppermute(moments, axes, spread(0, swap) + first_hop)  6.37 us
  transfers between devices with their start and end apart: 20, of which 8 were waited for; matrix products, arithmetic and copies ran while one was open for 9% of the time, Pallas kernels for 13%

profile of v3, /device:TPU:1, one launch (start us, length us, event | category | flops | bytes accessed | tf_op | source)
XLA Modules:
  0.0 199.6 jit_solution(6520514252015462581)
XLA Ops:
  0.6 0.7 iota_compare_fusion.2
  1.3 0.7 select_reduce_fusion.1
  2.0 0.1 select_reduce_fusion
  2.1 0.1 copy.14
  2.3 0.1 copy.15
  2.4 1.1 concatenate.3.refs_0_
  3.6 2.2 %collective-permute-start.171 = (bf16[192,1152]{1,0:T(8,128)(2,1)S(1)}, bf16[192,1152]{1,0:T(8,128)(2,1)S(1)}, u32[]{:S(2)}, u32[]{:S(2)}) collective-permute-start(bf16[192,1152]{1,0:T(8,128)(2,1)S(1)} %concatenate.3.refs_0_), channel_id=1, source_target_pairs={{0,2},{2,4},{4,6},{6,7},{7,5},{5,3},{3,1},{1,0},{8,10},{10,12},{12... | collective-permute-start | bytes 1327112 | tf_op jit(solution)/shard_map/ppermute | solution.py:186
  5.7 0.0 collective-permute-start.172
  5.7 9.8 %collective-permute-done.171.refs_1_ = bf16[192,1152]{1,0:T(8,128)(2,1)S(1)} collective-permute-done((bf16[192,1152]{1,0:T(8,128)(2,1)S(1)}, bf16[192,1152]{1,0:T(8,128)(2,1)S(1)}, u32[]{:S(2)}, u32[]{:S(2)}) %collective-permute-start.171) | collective-permute-done | bytes 442400 | tf_op jit(solution)/shard_map/ppermute | solution.py:186
  15.5 1.2 collective-permute-start.175
  16.8 0.0 collective-permute-done.172.refs_2_
  16.8 0.2 collective-permute-start.176
  17.0 7.5 %collective-permute-start.174 = (bf16[1,3,1024,256]{3,2,1,0:T(8,128)(2,1)}, bf16[1,3,1024,256]{3,2,1,0:T(8,128)(2,1)}, u32[]{:S(2)}, u32[]{:S(2)}) collective-permute-start(bf16[1,3,1024,256]{3,2,1,0:T(8,128)(2,1)} %refs_1_.1), channel_id=1, source_target_pairs={{0,16},{8,24},{16,0},{24,8},{1,17},{9,25},{17,1},{25,9},{2,18},{10... | collective-permute-start | bytes 4718600 | tf_op jit(solution)/shard_map/ppermute | solution.py:163
  24.5 1.3 select_reduce_fusion.3
  29.8 0.0 copy-start.5
  29.8 0.0 copy-start.6
  29.8 0.0 copy-start
  29.8 5.3 %shard_map.111 = bf16[2,3,1024,256]{3,2,1,0:T(8,128)(2,1)} custom-call(f32[1,3,1024,256]{3,2,1,0:T(8,128)} %first_ref.1, f32[1,3,1024,256]{3,2,1,0:T(8,128)} %second_ref.1), custom_call_target="tpu_custom_call" | custom-call | flops 786432 | bytes 9437184 | tf_op jit(solution)/shard_map/pallas_call | solution.py:70
  35.1 0.1 select_reduce_fusion.2
  35.3 0.0 collective-permute-done.175.refs_0_
  35.3 0.0 collective-permute-done.176.refs_1_
  35.3 103.5 %conditional.1 = (bf16[1,3,1024,256]{3,2,1,0:T(8,128)(2,1)}, bf16[2,3,1024,256]{3,2,1,0:T(8,128)(2,1)}, bf16[2,3,1024,256]{3,2,1,0:T(8,128)(2,1)}, bf16[192,1152...) conditional(s32[]{:T(128)} %clamp.3, ...), branch_computations={%region_6.7_spmd, %region_7.8_spmd, %region_8.9_spmd, %region_9.10... | conditional | flops 2581576 | bytes 56971744 | solution.py:98
  35.3 6.4 %collective-permute-start.49 = (bf16[2,3,1024,256]{3,2,1,0:T(8,128)(2,1)}, bf16[2,3,1024,256]{3,2,1,0:T(8,128)(2,1)}, u32[]{:S(2)}, u32[]{:S(2)}) collective-permute-start(bf16[2,3,1024,256]{3,2,1,0:T(8,128)(2,1)} %get-tuple-element.333), channel_id=1, source_target_pairs={{1,3},{3,1},{17,19},{19,17},{9,8},{11,10},{25,24},{27,26}} | collective-permute-start | bytes 9437192 | tf_op jit(solution)/shard_map/cond/branch_8_fun/ppermute | solution.py:42
  41.7 36.9 %collective-permute-done.49 = bf16[2,3,1024,256]{3,2,1,0:T(8,128)(2,1)} collective-permute-done((bf16[2,3,1024,256]{3,2,1,0:T(8,128)(2,1)}, bf16[2,3,1024,256]{3,2,1,0:T(8,128)(2,1)}, u32[]{:S(2)}, u32[]{:S(2)}) %collective-permute-start.49) | collective-permute-done | bytes 3145760 | tf_op jit(solution)/shard_map/cond/branch_8_fun/ppermute | solution.py:42
  78.7 4.1 %collective-permute-start.50 = (bf16[2,3,1024,256]{3,2,1,0:T(8,128)(2,1)}, bf16[2,3,1024,256]{3,2,1,0:T(8,128)(2,1)}, u32[]{:S(2)}, u32[]{:S(2)}) collective-permute-start(bf16[2,3,1024,256]{3,2,1,0:T(8,128)(2,1)} %collective-permute-done.49), channel_id=1, source_target_pairs={{8,11},{10,9},{24,27},{26,25}} | collective-permute-start | bytes 9437192 | tf_op jit(solution)/shard_map/cond/branch_8_fun/ppermute | solution.py:44
  82.7 3.7 %collective-permute-start.48 = (bf16[1,3,1024,256]{3,2,1,0:T(8,128)(2,1)S(1)}, bf16[1,3,1024,256]{3,2,1,0:T(8,128)(2,1)}, u32[]{:S(2)}, u32[]{:S(2)}) collective-permute-start(bf16[1,3,1024,256]{3,2,1,0:T(8,128)(2,1)S(1)} %get-tuple-element.332), channel_id=1, source_target_pairs={{1,3},{3,1},{17,19},{19,17},{9,11},{11,9},{25,27},{27,25}} | collective-permute-start | bytes 4718600 | tf_op jit(solution)/shard_map/cond/branch_8_fun/ppermute | solution.py:43
  86.4 1.4 collective-permute-start.51
  87.8 0.1 collective-permute-start.52
  87.9 37.1 %collective-permute-done.51 = bf16[192,1152]{1,0:T(8,128)(2,1)} collective-permute-done((bf16[192,1152]{1,0:T(8,128)(2,1)}, bf16[192,1152]{1,0:T(8,128)(2,1)}, u32[]{:S(2)}, u32[]{:S(2)}) %collective-permute-start.51) | collective-permute-done | bytes 442400 | tf_op jit(solution)/shard_map/cond/branch_8_fun/ppermute | solution.py:192
  125.0 0.8 collective-permute-done.52
  125.8 1.1 broadcast_select_fusion.8
  126.8 6.7 %collective-permute-start.53 = (bf16[192,1152]{1,0:T(8,128)(2,1)S(1)}, bf16[192,1152]{1,0:T(8,128)(2,1)}, u32[]{:S(2)}, u32[]{:S(2)}) collective-permute-start(bf16[192,1152]{1,0:T(8,128)(2,1)S(1)} %broadcast_select_fusion.8), channel_id=1, source_target_pairs={{0,2},{2,4},{4,6},{6,7},{7,5},{5,3},{3,1},{1,0},{10,8},{12,10},{14... | collective-permute-start | bytes 1327112 | tf_op jit(solution)/shard_map/cond/branch_8_fun/ppermute | solution.py:196
  133.5 5.2 %collective-permute-done.53 = bf16[192,1152]{1,0:T(8,128)(2,1)} collective-permute-done((bf16[192,1152]{1,0:T(8,128)(2,1)S(1)}, bf16[192,1152]{1,0:T(8,128)(2,1)}, u32[]{:S(2)}, u32[]{:S(2)}) %collective-permute-start.53) | collective-permute-done | bytes 442400 | tf_op jit(solution)/shard_map/cond/branch_8_fun/ppermute | solution.py:196
  138.8 0.0 collective-permute-done.48
  138.8 0.0 collective-permute-done.50
  138.8 2.5 %collective-permute-start.173 = (bf16[1,3,1024,256]{3,2,1,0:T(8,128)(2,1)S(1)}, bf16[1,3,1024,256]{3,2,1,0:T(8,128)(2,1)S(1)}, u32[]{:S(2)}, u32[]{:S(2)}) collective-permute-start(bf16[1,3,1024,256]{3,2,1,0:T(8,128)(2,1)S(1)} %copy-done), channel_id=1, source_target_pairs={{0,8},{8,0},{16,24},{24,16},{1,9},{9,1},{17,25},{25,17},{2,10},{10... | collective-permute-start | bytes 4718600 | tf_op jit(solution)/shard_map/ppermute | solution.py:214
  141.2 3.0 %collective-permute-done.173.refs_4_.refs_3_.refs_2_ = bf16[1,3,1024,256]{3,2,1,0:T(8,128)(2,1)S(1)} collective-permute-done((bf16[1,3,1024,256]{3,2,1,0:T(8,128)(2,1)S(1)}, bf16[1,3,1024,256]{3,2,1,0:T(8,128)(2,1)S(1)}, u32[]{:S(2)}, u32[]{:S(2)}) %collective-permute-start.173) | collective-permute-done | bytes 1572896 | tf_op jit(solution)/shard_map/ppermute | solution.py:214
  144.3 0.4 collective-permute-start.177
  144.7 3.4 %collective-permute-done.177.refs_6_.refs_5_.refs_4_ = bf16[1,3,1024,256]{3,2,1,0:T(8,128)(2,1)} collective-permute-done((bf16[1,3,1024,256]{3,2,1,0:T(8,128)(2,1)}, bf16[1,3,1024,256]{3,2,1,0:T(8,128)(2,1)}, u32[]{:S(2)}, u32[]{:S(2)}) %collective-permute-start.177) | collective-permute-done | bytes 1572896 | tf_op jit(solution)/shard_map/ppermute | solution.py:218
  148.0 5.1 %shard_map.115 = bf16[192,1024]{1,0:T(8,128)(2,1)} custom-call(s32[1]{0:T(128)} %bitcast.4.slot_ref, bf16[192,1152]{1,0:T(8,128)(2,1)} %get-tuple-element.471.refs_0_, bf16[1,3,1024,256]{3,2,1,0:T(8,128)(2,1)S(1)} %copy-done, bf16[1,3,1024,256]{3,2,1,0:T(8,128)(2,1)} %copy-done.2, bf16[1,3,1024,256]{3,2,1,0:T(8,128)(2,1)} %collective-permute-done.174.refs_5_.refs_4_.refs_3_, ...), custom_call_target="tpu_custom_call" | custom-call | flops 1207959552 | bytes 7471104 | tf_op jit(solution)/shard_map/pallas_call | solution.py:134
  153.2 1.7 collective-permute-start.178
  154.9 6.5 %shard_map.114 = (f32[192,1024]{1,0:T(8,128)}, f32[192,1024]{1,0:T(8,128)}) custom-call(s32[1]{0:T(128)} %bitcast.4.slot_ref, bf16[192,1152]{1,0:T(8,128)(2,1)} %get-tuple-element.468.refs_0_, bf16[192,1152]{1,0:T(8,128)(2,1)} %get-tuple-element.469.refs_1_, bf16[1,3,1024,256]{3,2,1,0:T(8,128)(2,1)S(1)} %copy-done, bf16[1,3,1024,256]{3,2,1,0:T(8,128)(2,1)} %copy-done.2, ...), custom_call_target="tpu_custom_call" | custom-call | flops 2415919104 | bytes 8650752 | tf_op jit(solution)/shard_map/pallas_call | solution.py:134
  161.4 0.0 collective-permute-done.178
  161.4 1.6 fusion.1
  163.0 0.6 collective-permute-start.179
  163.7 0.6 fusion.4
  165.0 0.9 collective-permute-start.182
  165.9 6.6 %shard_map.113 = (f32[192,1024]{1,0:T(8,128)}, f32[192,1024]{1,0:T(8,128)}) custom-call(s32[1]{0:T(128)} %bitcast.4.slot_ref, bf16[192,1152]{1,0:T(8,128)(2,1)} %collective-permute-done.175.refs_0_, bf16[192,1152]{1,0:T(8,128)(2,1)} %collective-permute-done.176.refs_1_, bf16[1,3,1024,256]{3,2,1,0:T(8,128)(2,1)S(1)} %copy-done, ...), custom_call_target="tpu_custom_call" | custom-call | flops 2415919104 | bytes 8650752 | tf_op jit(solution)/shard_map/pallas_call | solution.py:134
  172.5 1.2 collective-permute-done.179
  173.7 1.2 add_convert_fusion.4
  174.9 0.1 collective-permute-start.180
  175.0 0.0 collective-permute-done.182
  175.0 1.2 add_convert_fusion.2
  176.2 1.5 collective-permute-start.183
  177.7 7.9 %shard_map.112 = (f32[192,1024]{1,0:T(8,128)}, f32[192,1024]{1,0:T(8,128)}, f32[192,1024]{1,0:T(8,128)}) custom-call(s32[1]{0:T(128)} %bitcast.4.slot_ref, bf16[192,1152]{1,0:T(8,128)(2,1)} %copy-done.4, bf16[192,1152]{1,0:T(8,128)(2,1)} %copy-done.7, bf16[192,1152]{1,0:T(8,128)(2,1)} %copy-done.8, bf16[1,3,1024,256]{3,2,1,0:T(8,128)(2,1)S(1)} %copy-done, ...), custom_call_target="tpu_custom_call" | custom-call | flops 3623878656 | bytes 9830400 | tf_op jit(solution)/shard_map/pallas_call | solution.py:134
  185.6 0.0 collective-permute-done.180
  185.6 1.4 add_convert_fusion.3
  187.0 0.1 collective-permute-start.181
  187.1 0.0 collective-permute-done.183
  187.1 1.2 add_convert_fusion.1
  188.3 1.5 collective-permute-start.184
  189.8 7.5 %convert_select_fusion = (f32[1,3,1024,256]{3,2,1,0:T(8,128)}, f32[1,3,1024,256]{3,2,1,0:T(8,128)}) fusion(f32[1,3,1024,256]{3,2,1,0:T(8,128)} %second_ref.1, bf16[2,3,1024,256]{3,2,1,0:T(8,128)(2,1)} %get-tuple-element.477, bf16[2,3,1024,256]{3,2,1,0:T(8,128)(2,1)} %get-tuple-element.476, pred[]{:T(512)} %eq.65, pred[]{:T(512)S(6)} %ne.24, ...), kind=kLoop, calls=%fused_computation.36 | loop fusion | flops 4718592 | bytes 18874370 | tf_op jit(solution)/shard_map/jit(_where)/select_n | solution.py:244
  197.4 1.3 broadcast_select_fusion.31
  198.7 0.9 add_convert_fusion
  (20 shorter events, 0.1 us)
Async XLA Ops:
  3.5 26.2 %copy-start.4 = (bf16[192,1152]{1,0:T(8,128)(2,1)}, bf16[192,1152]{1,0:T(8,128)(2,1)S(1)}, u32[]{:S(2)}) copy-start(bf16[192,1152]{1,0:T(8,128)(2,1)S(1)} %concatenate.3.refs_0_) | copy-start | bytes 1327108
  3.6 12.0 %collective-permute-start.171 = (bf16[192,1152]{1,0:T(8,128)(2,1)S(1)}, bf16[192,1152]{1,0:T(8,128)(2,1)S(1)}, u32[]{:S(2)}, u32[]{:S(2)}) collective-permute-start(bf16[192,1152]{1,0:T(8,128)(2,1)S(1)} %concatenate.3.refs_0_), channel_id=1, source_target_pairs={{0,2},{2,4},{4,6},{6,7},{7,5},{5,3},{3,1},{1,0},{8,10},{10,12},{12... | collective-permute-start | bytes 1327112 | tf_op jit(solution)/shard_map/ppermute | solution.py:186
  5.7 11.1 %collective-permute-start.172 = (bf16[192,1152]{1,0:T(8,128)(2,1)S(1)}, bf16[192,1152]{1,0:T(8,128)(2,1)S(1)}, u32[]{:S(2)}, u32[]{:S(2)}) collective-permute-start(bf16[192,1152]{1,0:T(8,128)(2,1)S(1)} %concatenate.3.refs_0_), channel_id=1, source_target_pairs={{2,0},{4,2},{6,4},{7,6},{5,7},{3,5},{1,3},{0,1},{10,8},{12,10},{14... | collective-permute-start | bytes 1327112 | tf_op jit(solution)/shard_map/ppermute | solution.py:187
  15.5 19.6 %copy-start.7 = (bf16[192,1152]{1,0:T(8,128)(2,1)}, bf16[192,1152]{1,0:T(8,128)(2,1)S(1)}, u32[]{:S(2)}) copy-start(bf16[192,1152]{1,0:T(8,128)(2,1)S(1)} %collective-permute-done.171.refs_1_) | copy-start | bytes 1327108
  15.5 19.7 %collective-permute-start.175 = (bf16[192,1152]{1,0:T(8,128)(2,1)S(1)}, bf16[192,1152]{1,0:T(8,128)(2,1)}, u32[]{:S(2)}, u32[]{:S(2)}) collective-permute-start(bf16[192,1152]{1,0:T(8,128)(2,1)S(1)} %collective-permute-done.171.refs_1_), channel_id=1, source_target_pairs={{0,2},{2,4},{4,6},{6,7},{7,5},{5,3},{3,1},{1,0},{8,10},{10,12},{12... | collective-permute-start | bytes 1327112 | tf_op jit(solution)/shard_map/ppermute | solution.py:186
  16.8 18.3 %copy-start.8 = (bf16[192,1152]{1,0:T(8,128)(2,1)}, bf16[192,1152]{1,0:T(8,128)(2,1)S(1)}, u32[]{:S(2)}) copy-start(bf16[192,1152]{1,0:T(8,128)(2,1)S(1)} %collective-permute-done.172.refs_2_) | copy-start | bytes 1327108
  16.8 18.5 %collective-permute-start.176 = (bf16[192,1152]{1,0:T(8,128)(2,1)S(1)}, bf16[192,1152]{1,0:T(8,128)(2,1)}, u32[]{:S(2)}, u32[]{:S(2)}) collective-permute-start(bf16[192,1152]{1,0:T(8,128)(2,1)S(1)} %collective-permute-done.172.refs_2_), channel_id=1, source_target_pairs={{2,0},{4,2},{6,4},{7,6},{5,7},{3,5},{1,3},{0,1},{10,8},{12,10},{14... | collective-permute-start | bytes 1327112 | tf_op jit(solution)/shard_map/ppermute | solution.py:187
  17.0 124.2 %collective-permute-start.174 = (bf16[1,3,1024,256]{3,2,1,0:T(8,128)(2,1)}, bf16[1,3,1024,256]{3,2,1,0:T(8,128)(2,1)}, u32[]{:S(2)}, u32[]{:S(2)}) collective-permute-start(bf16[1,3,1024,256]{3,2,1,0:T(8,128)(2,1)} %refs_1_.1), channel_id=1, source_target_pairs={{0,16},{8,24},{16,0},{24,8},{1,17},{9,25},{17,1},{25,9},{2,18},{10... | collective-permute-start | bytes 4718600 | tf_op jit(solution)/shard_map/ppermute | solution.py:163
  29.8 5.3 %copy-start.5 = (s32[8]{0:T(128)S(1)}, s32[8]{0:T(128)}, u32[]{:S(2)}) copy-start(s32[8]{0:T(128)} %param.40) | copy-start | bytes 100
  29.8 5.3 %copy-start.6 = (s32[8]{0:T(128)S(1)}, s32[8]{0:T(128)}, u32[]{:S(2)}) copy-start(s32[8]{0:T(128)} %param.41) | copy-start | bytes 100
  29.8 5.5 %copy-start = (bf16[1,3,1024,256]{3,2,1,0:T(8,128)(2,1)S(1)}, bf16[1,3,1024,256]{3,2,1,0:T(8,128)(2,1)}, u32[]{:S(2)}) copy-start(bf16[1,3,1024,256]{3,2,1,0:T(8,128)(2,1)} %refs_1_.1) | copy-start | bytes 4718596
  35.3 43.3 %collective-permute-start.49 = (bf16[2,3,1024,256]{3,2,1,0:T(8,128)(2,1)}, bf16[2,3,1024,256]{3,2,1,0:T(8,128)(2,1)}, u32[]{:S(2)}, u32[]{:S(2)}) collective-permute-start(bf16[2,3,1024,256]{3,2,1,0:T(8,128)(2,1)} %get-tuple-element.333), channel_id=1, source_target_pairs={{1,3},{3,1},{17,19},{19,17},{9,8},{11,10},{25,24},{27,26}} | collective-permute-start | bytes 9437192 | tf_op jit(solution)/shard_map/cond/branch_8_fun/ppermute | solution.py:42
  78.7 60.1 %collective-permute-start.50 = (bf16[2,3,1024,256]{3,2,1,0:T(8,128)(2,1)}, bf16[2,3,1024,256]{3,2,1,0:T(8,128)(2,1)}, u32[]{:S(2)}, u32[]{:S(2)}) collective-permute-start(bf16[2,3,1024,256]{3,2,1,0:T(8,128)(2,1)} %collective-permute-done.49), channel_id=1, source_target_pairs={{8,11},{10,9},{24,27},{26,25}} | collective-permute-start | bytes 9437192 | tf_op jit(solution)/shard_map/cond/branch_8_fun/ppermute | solution.py:44
  82.7 56.1 %collective-permute-start.48 = (bf16[1,3,1024,256]{3,2,1,0:T(8,128)(2,1)S(1)}, bf16[1,3,1024,256]{3,2,1,0:T(8,128)(2,1)}, u32[]{:S(2)}, u32[]{:S(2)}) collective-permute-start(bf16[1,3,1024,256]{3,2,1,0:T(8,128)(2,1)S(1)} %get-tuple-element.332), channel_id=1, source_target_pairs={{1,3},{3,1},{17,19},{19,17},{9,11},{11,9},{25,27},{27,25}} | collective-permute-start | bytes 4718600 | tf_op jit(solution)/shard_map/cond/branch_8_fun/ppermute | solution.py:43
  86.4 38.6 %collective-permute-start.51 = (bf16[192,1152]{1,0:T(8,128)(2,1)}, bf16[192,1152]{1,0:T(8,128)(2,1)}, u32[]{:S(2)}, u32[]{:S(2)}) collective-permute-start(bf16[192,1152]{1,0:T(8,128)(2,1)} %get-tuple-element.334), channel_id=1, source_target_pairs={{0,2},{2,4},{4,6},{6,7},{7,5},{5,3},{3,1},{1,0},{8,10},{10,12},{12... | collective-permute-start | bytes 1327112 | tf_op jit(solution)/shard_map/cond/branch_8_fun/ppermute | solution.py:192
  87.8 38.0 %collective-permute-start.52 = (bf16[192,1152]{1,0:T(8,128)(2,1)}, bf16[192,1152]{1,0:T(8,128)(2,1)}, u32[]{:S(2)}, u32[]{:S(2)}) collective-permute-start(bf16[192,1152]{1,0:T(8,128)(2,1)} %get-tuple-element.335), channel_id=1, source_target_pairs={{2,0},{4,2},{6,4},{7,6},{5,7},{3,5},{1,3},{0,1},{10,8},{12,10},{14... | collective-permute-start | bytes 1327112 | tf_op jit(solution)/shard_map/cond/branch_8_fun/ppermute | solution.py:193
  126.8 11.9 %collective-permute-start.53 = (bf16[192,1152]{1,0:T(8,128)(2,1)S(1)}, bf16[192,1152]{1,0:T(8,128)(2,1)}, u32[]{:S(2)}, u32[]{:S(2)}) collective-permute-start(bf16[192,1152]{1,0:T(8,128)(2,1)S(1)} %broadcast_select_fusion.8), channel_id=1, source_target_pairs={{0,2},{2,4},{4,6},{6,7},{7,5},{5,3},{3,1},{1,0},{10,8},{12,10},{14... | collective-permute-start | bytes 1327112 | tf_op jit(solution)/shard_map/cond/branch_8_fun/ppermute | solution.py:196
  138.8 5.5 %collective-permute-start.173 = (bf16[1,3,1024,256]{3,2,1,0:T(8,128)(2,1)S(1)}, bf16[1,3,1024,256]{3,2,1,0:T(8,128)(2,1)S(1)}, u32[]{:S(2)}, u32[]{:S(2)}) collective-permute-start(bf16[1,3,1024,256]{3,2,1,0:T(8,128)(2,1)S(1)} %copy-done), channel_id=1, source_target_pairs={{0,8},{8,0},{16,24},{24,16},{1,9},{9,1},{17,25},{25,17},{2,10},{10... | collective-permute-start | bytes 4718600 | tf_op jit(solution)/shard_map/ppermute | solution.py:214
  144.3 3.8 %copy-start.2 = (bf16[1,3,1024,256]{3,2,1,0:T(8,128)(2,1)}, bf16[1,3,1024,256]{3,2,1,0:T(8,128)(2,1)S(1)}, u32[]{:S(2)}) copy-start(bf16[1,3,1024,256]{3,2,1,0:T(8,128)(2,1)S(1)} %collective-permute-done.173.refs_4_.refs_3_.refs_2_) | copy-start | bytes 4718596
  144.3 3.8 %collective-permute-start.177 = (bf16[1,3,1024,256]{3,2,1,0:T(8,128)(2,1)}, bf16[1,3,1024,256]{3,2,1,0:T(8,128)(2,1)}, u32[]{:S(2)}, u32[]{:S(2)}) collective-permute-start(bf16[1,3,1024,256]{3,2,1,0:T(8,128)(2,1)} %collective-permute-done.174.refs_5_.refs_4_.refs_3_), channel_id=1, source_target_pairs={{0,8},{8,0},{16,24},{24,16},{1,9},{9,1},{17,25},{25,17},{2,10},{10... | collective-permute-start | bytes 4718600 | tf_op jit(solution)/shard_map/ppermute | solution.py:218
  153.2 8.3 %collective-permute-start.178 = (bf16[192,1024]{1,0:T(8,128)(2,1)}, bf16[192,1024]{1,0:T(8,128)(2,1)S(1)}, u32[]{:S(2)}, u32[]{:S(2)}) collective-permute-start(bf16[192,1024]{1,0:T(8,128)(2,1)} %shard_map.115), channel_id=1, source_target_pairs={{0,2},{2,4},{4,6},{6,7},{7,5},{5,3},{3,1},{1,0},{10,8},{12,10},{14... | collective-permute-start | bytes 1179656 | tf_op jit(solution)/shard_map/ppermute | solution.py:230
  163.0 10.7 %collective-permute-start.179 = (bf16[192,1024]{1,0:T(8,128)(2,1)S(1)}, bf16[192,1024]{1,0:T(8,128)(2,1)S(1)}, u32[]{:S(2)}, u32[]{:S(2)}) collective-permute-start(bf16[192,1024]{1,0:T(8,128)(2,1)S(1)} %get-tuple-element.485), channel_id=1, source_target_pairs={{2,0},{4,2},{6,4},{7,6},{5,7},{3,5},{1,3},{0,1},{10,8},{12,10},{14... | collective-permute-start | bytes 1179656 | tf_op jit(solution)/shard_map/ppermute | solution.py:236
  165.0 10.0 %collective-permute-start.182 = (bf16[192,1024]{1,0:T(8,128)(2,1)S(1)}, bf16[192,1024]{1,0:T(8,128)(2,1)S(1)}, u32[]{:S(2)}, u32[]{:S(2)}) collective-permute-start(bf16[192,1024]{1,0:T(8,128)(2,1)S(1)} %get-tuple-element.486), channel_id=1, source_target_pairs={{0,2},{2,4},{4,6},{6,7},{7,5},{5,3},{3,1},{1,0},{8,10},{10,12},{12... | collective-permute-start | bytes 1179656 | tf_op jit(solution)/shard_map/ppermute | solution.py:237
  174.9 10.7 %collective-permute-start.180 = (bf16[192,1024]{1,0:T(8,128)(2,1)S(1)}, bf16[192,1024]{1,0:T(8,128)(2,1)S(1)}, u32[]{:S(2)}, u32[]{:S(2)}) collective-permute-start(bf16[192,1024]{1,0:T(8,128)(2,1)S(1)} %add_convert_fusion.4), channel_id=1, source_target_pairs={{2,0},{4,2},{6,4},{7,6},{5,7},{3,5},{1,3},{0,1},{10,8},{12,10},{14... | collective-permute-start | bytes 1179656 | tf_op jit(solution)/shard_map/ppermute | solution.py:236
  176.2 10.9 %collective-permute-start.183 = (bf16[192,1024]{1,0:T(8,128)(2,1)S(1)}, bf16[192,1024]{1,0:T(8,128)(2,1)S(1)}, u32[]{:S(2)}, u32[]{:S(2)}) collective-permute-start(bf16[192,1024]{1,0:T(8,128)(2,1)S(1)} %add_convert_fusion.2), channel_id=1, source_target_pairs={{0,2},{2,4},{4,6},{6,7},{7,5},{5,3},{3,1},{1,0},{8,10},{10,12},{12... | collective-permute-start | bytes 1179656 | tf_op jit(solution)/shard_map/ppermute | solution.py:237
  185.6 4.2 %copy-start.1 = (f32[1,3,1024,256]{3,2,1,0:T(8,128)S(1)}, f32[1,3,1024,256]{3,2,1,0:T(8,128)}, u32[]{:S(2)}) copy-start(f32[1,3,1024,256]{3,2,1,0:T(8,128)} %first_ref.1) | copy-start | bytes 9437188
  187.0 11.6 %collective-permute-start.181 = (bf16[192,1024]{1,0:T(8,128)(2,1)S(1)}, bf16[192,1024]{1,0:T(8,128)(2,1)S(1)}, u32[]{:S(2)}, u32[]{:S(2)}) collective-permute-start(bf16[192,1024]{1,0:T(8,128)(2,1)S(1)} %add_convert_fusion.3), channel_id=1, source_target_pairs={{2,0},{4,2},{6,4},{7,6},{5,7},{3,5},{1,3},{0,1},{10,8},{12,10},{14... | collective-permute-start | bytes 1179656 | tf_op jit(solution)/shard_map/ppermute | solution.py:236
  188.3 10.3 %collective-permute-start.184 = (bf16[192,1024]{1,0:T(8,128)(2,1)S(1)}, bf16[192,1024]{1,0:T(8,128)(2,1)S(1)}, u32[]{:S(2)}, u32[]{:S(2)}) collective-permute-start(bf16[192,1024]{1,0:T(8,128)(2,1)S(1)} %add_convert_fusion.1), channel_id=1, source_target_pairs={{0,2},{2,4},{4,6},{6,7},{7,5},{5,3},{3,1},{1,0},{8,10},{10,12},{12... | collective-permute-start | bytes 1179656 | tf_op jit(solution)/shard_map/ppermute | solution.py:237
  197.4 1.3 copy-start.3

commit v4 on v3

--- a/solution.py
+++ b/solution.py
@@ -79,23 +79,24 @@
     )(first_moment, second_moment)
 
 
-def relocate(weights, packed, ring, finish, old_owner, new_owner, source_slot, dp_count, count):
+def relocate(weights, packed, fetch, old_owner, new_owner, source_slot, dp_count, count):
     pairs = list(itertools.combinations(range(count), 2))
     if len(pairs) > PAIR_LIMIT:
-        return any_permutation(source_slot, weights, packed), finish(*ring)
+        return any_permutation(source_slot, weights, packed), fetch(weights)
+    pairs.sort(key=lambda pair: pair[::-1])
     differs = old_owner != new_owner
     low = jnp.min(jnp.where(differs, old_owner, count))
     high = jnp.max(jnp.where(differs, old_owner, 0))
-    number = low * count - low * (low + 1) // 2 + high - low - 1
+    number = lax.shift_right_logical(high * (high - 1), 1) + low
     branch = jnp.where(jnp.sum(differs.astype(jnp.int32)) == 2, number, len(pairs))
 
-    def moving(pair, weights, packed, ring):
-        return swap_slots(pair, dp_count, count, weights, packed), finish(*ring)
+    def moving(pair, weights, packed):
+        return swap_slots(pair, dp_count, count, weights, packed), fetch(weights)
 
     branches = [functools.partial(moving, pair) for pair in pairs] + [
-        lambda weights, packed, ring: (any_permutation(source_slot, weights, packed), finish(*ring))
+        lambda weights, packed: (any_permutation(source_slot, weights, packed), fetch(weights))
     ]
-    return lax.switch(branch, branches, weights, packed, ring)
+    return lax.switch(branch, branches, weights, packed)
 
 
 def expert_kernel(blocks, shards, width, count, slot_ref, *refs):
@@ -149,18 +150,20 @@
 ):
     count, dp_count = lax.axis_size("expert"), lax.axis_size("dp")
     tok_rows, width = tokens.shape
-    odd = lax.axis_index("dp") % 2 == 1
+    odd = lax.bitwise_and(lax.axis_index("dp"), 1) == 1
     labels = jnp.arange(count, dtype=jnp.int32)
     source_slot = jnp.sum(
         jnp.where(new_owner[None, :] == labels[:, None], old_owner[None, :], 0), axis=1
     )
     slot = lax.axis_index("expert").astype(jnp.int32)
 
-    swap = [(i, i ^ 1) for i in range(dp_count)]
-    far = []
-    for step in range(1, dp_count // 2):
-        turn = [(i, (i + 2 * step) % dp_count) for i in range(dp_count)]
-        far.append(lax.ppermute(weights, "dp", turn))
+    def fetch(block):
+        shards = []
+        for step in range(1, dp_count // 2):
+            turn = [(i, (i + 2 * step) % dp_count) for i in range(dp_count)]
+            shards.append(lax.ppermute(block, "dp", turn))
+        return shards
+
     by_expert = jnp.sum(
         jnp.where(route_ids[:, :, None] == labels[None, None, :], gate_weight[:, :, None], 0.0),
         axis=1,
@@ -180,52 +183,41 @@
         for row in range(dp_count)
         for a, b in (behind if row % 2 else ahead)
     ]
+    swap = [(i, i ^ 1) for i in range(dp_count)]
     steps = count // 2
     from_behind, from_ahead = [packed], [packed]
-    for _ in range(1, min(3, steps)):
+
+    def hop():
         from_behind.append(lax.ppermute(from_behind[-1], "expert", ahead))
         from_ahead.append(lax.ppermute(from_ahead[-1], "expert", behind))
 
-    def finish(back, front):
-        backs, fronts = [], []
-        for _ in range(3, steps):
-            back = lax.ppermute(back, "expert", ahead)
-            front = lax.ppermute(front, "expert", behind)
-            backs.append(back)
-            fronts.append(front)
-        outer = lax.ppermute(jnp.where(odd, front, back), ("dp", "expert"), opposite)
-        return backs, fronts, outer
-
+    hop()
+    shards = [weights, lax.ppermute(weights, "dp", swap)]
     moments = pack_moments(first_moment, second_moment)
-    moved, (backs, fronts, farthest) = relocate(
-        weights,
-        moments,
-        (from_behind[-1], from_ahead[-1]),
-        finish,
-        old_owner,
-        new_owner,
-        source_slot,
-        dp_count,
-        count,
-    )
-    from_behind += backs
-    from_ahead += fronts
-    far, moved = lax.optimization_barrier((far, moved))
-    near = lax.ppermute(weights, "dp", swap)
-    shards = [weights, near]
+    moved, far = relocate(
+        weights, moments, fetch, old_owner, new_owner, source_slot, dp_count, count
+    )
+    moved, from_behind[1], from_ahead[1] = lax.optimization_barrier(
+        (moved, from_behind[1], from_ahead[1])
+    )
     for shard in far:
-        shard, near = lax.optimization_barrier((shard, near))
-        near = lax.ppermute(shard, "dp", swap)
-        shards += [shard, near]
+        shard, shards[-1] = lax.optimization_barrier((shard, shards[-1]))
+        shards += [shard, lax.ppermute(shard, "dp", swap)]
 
     apply = functools.partial(
         run_expert, slot.reshape(1), shards=shards, width=width, count=count
     )
+    answers = {}
+    for _ in range(2, steps):
+        hop()
+    for step in range(1, steps):
+        blocks = [from_behind[step], from_ahead[step]] + ([packed] if step == 1 else [])
+        answers[step] = list(apply(blocks, jnp.float32))
+    own = answers[1].pop()
+    farthest = lax.ppermute(
+        jnp.where(odd, from_ahead[-1], from_behind[-1]), ("dp", "expert"), opposite
+    )
     (outermost,) = apply([farthest], jnp.bfloat16)
-    answers = {}
-    for step in range(steps - 1, 1, -1):
-        answers[step] = apply([from_behind[step], from_ahead[step]], jnp.float32)
-    own, *answers[1] = apply([packed, from_behind[1], from_ahead[1]], jnp.float32)
 
     arrived = lax.ppermute(outermost, ("dp", "expert"), opposite).astype(jnp.float32)
     to_behind, to_ahead = jnp.where(odd, arrived, 0.0), jnp.where(odd, 0.0, arrived)

time: 202 us -> 200 us (0.990)
  the two profiles are of different devices: /device:TPU:1 before, /device:TPU:0 now
where the time goes in v4:
time: 200 us
  waiting for transfers between devices  70.5 us (35%)
  starting transfers between devices  69.6 us (35%)
  Pallas kernels  31.4 us (16%)
  other arithmetic  20.7 us (10%)
  between operations  4.03 us (2%)
  local copies, waits for them, and re-layouts  3.33 us (2%)
    ppermute x1, starting transfers between devices, swap_slots(): lax.ppermute(weights, axes, spread(0, swap) + spread(1, swap))  40.7 us
    ppermute x1, waiting for transfers between devices, fetch(): shards.append(lax.ppermute(block, 'dp', turn))  34.9 us
    pallas_call x4, Pallas kernels, run_expert(): pl.pallas_call(functools.partial(expert_kernel, blocks, len(shards), widt...  26.2 us
    ppermute x3, waiting for transfers between devices, hop(): from_behind.append(lax.ppermute(from_behind[-1], 'expert', ahead))  17.2 us
    ppermute x3, waiting for transfers between devices, hop(): from_ahead.append(lax.ppermute(from_ahead[-1], 'expert', behind))  11.2 us
    select_n x1, other arithmetic, whole(): jnp.where(here, jnp.where(odd, relayed[i], direct[i]).astype(m.dtype), m[0])  7.53 us
    ppermute x1, waiting for transfers between devices, whole(): lax.ppermute(jnp.where(odd, from_ahead[-1], from_behind[-1]), ('dp', 'exp...  7.15 us
    ppermute x1, starting transfers between devices, swap_slots(): direct = lax.ppermute(moments, axes, spread(0, swap) + first_hop)  6.96 us
  transfers between devices with their start and end apart: 20, of which 6 were waited for; matrix products, arithmetic and copies ran while one was open for 10% of the time, Pallas kernels for 13%

profile of v4, /device:TPU:0, one launch (start us, length us, event | category | flops | bytes accessed | tf_op | source)
XLA Modules:
  0.0 199.6 jit_solution(7273549051068467276)
XLA Ops:
  0.6 0.6 collective-permute-start.115
  1.2 0.7 select_reduce_fusion.1
  1.9 0.7 iota_compare_fusion.1
  2.6 0.1 select_reduce_fusion
  2.7 0.1 copy.14
  2.8 0.1 copy.15
  3.0 1.9 concatenate.3.refs_2_
  4.8 2.6 %collective-permute-start.113 = (bf16[192,1152]{1,0:T(8,128)(2,1)}, bf16[192,1152]{1,0:T(8,128)(2,1)}, u32[]{:S(2)}, u32[]{:S(2)}) collective-permute-start(bf16[192,1152]{1,0:T(8,128)(2,1)} %concatenate.3.refs_2_), channel_id=1, source_target_pairs={{0,2},{2,4},{4,6},{6,7},{7,5},{5,3},{3,1},{1,0},{8,10},{10,12},{12... | collective-permute-start | bytes 1327112 | tf_op jit(solution)/shard_map/ppermute | solution.py:191
  7.4 1.3 select_reduce_fusion.3
  10.1 0.0 copy-start.5
  10.1 0.0 copy-start.6
  10.1 0.0 copy-start
  10.1 5.3 %shard_map.111 = bf16[2,3,1024,256]{3,2,1,0:T(8,128)(2,1)} custom-call(f32[1,3,1024,256]{3,2,1,0:T(8,128)} %first_ref.1, f32[1,3,1024,256]{3,2,1,0:T(8,128)} %second_ref.1), custom_call_target="tpu_custom_call" | custom-call | flops 786432 | bytes 9437184 | tf_op jit(solution)/shard_map/pallas_call | solution.py:70
  15.4 0.1 select_reduce_fusion.2
  16.8 86.8 %conditional.1 = (bf16[1,3,1024,256]{3,2,1,0:T(8,128)(2,1)}, bf16[2,3,1024,256]{3,2,1,0:T(8,128)(2,1)}, bf16[2,3,1024,256]{3,2,1,0:T(8,128)(2,1)}, bf16[1,3,1024,256]{3,2,1,0:T(8,128)(2,1)}) conditional(s32[]{:T(128)} %clamp.3, (bf16[1,3,1024,256]{3,2,1,0:T(8,128)(2,1)S(1)}, ...), branch_computations={%region_4.5_spmd, %region_5.6_spmd, %region_6.7_spmd, %region_7.8_... | conditional | flops 2360392 | bytes 56627584 | solution.py:99
  16.9 7.0 %collective-permute-start.17 = (bf16[2,3,1024,256]{3,2,1,0:T(8,128)(2,1)}, bf16[2,3,1024,256]{3,2,1,0:T(8,128)(2,1)}, u32[]{:S(2)}, u32[]{:S(2)}) collective-permute-start(bf16[2,3,1024,256]{3,2,1,0:T(8,128)(2,1)} %get-tuple-element.127), channel_id=1, source_target_pairs={{1,3},{3,1},{17,19},{19,17},{9,8},{11,10},{25,24},{27,26}} | collective-permute-start | bytes 9437192 | tf_op jit(solution)/shard_map/cond/branch_4_fun/ppermute | solution.py:42
  23.8 0.0 collective-permute-done.17
  23.8 2.4 %collective-permute-start.18 = (bf16[2,3,1024,256]{3,2,1,0:T(8,128)(2,1)}, bf16[2,3,1024,256]{3,2,1,0:T(8,128)(2,1)}, u32[]{:S(2)}, u32[]{:S(2)}) collective-permute-start(bf16[2,3,1024,256]{3,2,1,0:T(8,128)(2,1)} %collective-permute-done.17), channel_id=1, source_target_pairs={{8,11},{10,9},{24,27},{26,25}} | collective-permute-start | bytes 9437192 | tf_op jit(solution)/shard_map/cond/branch_4_fun/ppermute | solution.py:44
  26.2 40.7 %collective-permute-start.16 = (bf16[1,3,1024,256]{3,2,1,0:T(8,128)(2,1)S(1)}, bf16[1,3,1024,256]{3,2,1,0:T(8,128)(2,1)}, u32[]{:S(2)}, u32[]{:S(2)}) collective-permute-start(bf16[1,3,1024,256]{3,2,1,0:T(8,128)(2,1)S(1)} %get-tuple-element.126), channel_id=1, source_target_pairs={{1,3},{3,1},{17,19},{19,17},{9,11},{11,9},{25,27},{27,25}} | collective-permute-start | bytes 4718600 | tf_op jit(solution)/shard_map/cond/branch_4_fun/ppermute | solution.py:43
  66.9 1.9 collective-permute-start.19
  68.8 0.0 collective-permute-done.16
  68.8 34.9 %collective-permute-done.19 = bf16[1,3,1024,256]{3,2,1,0:T(8,128)(2,1)} collective-permute-done((bf16[1,3,1024,256]{3,2,1,0:T(8,128)(2,1)S(1)}, bf16[1,3,1024,256]{3,2,1,0:T(8,128)(2,1)}, u32[]{:S(2)}, u32[]{:S(2)}) %collective-permute-start.19) | collective-permute-done | bytes 1572896 | tf_op jit(solution)/shard_map/cond/branch_4_fun/ppermute | solution.py:164
  103.7 0.0 collective-permute-done.18
  103.7 1.1 collective-permute-start.114
  104.8 0.0 collective-permute-done.113.refs_0_
  104.8 10.6 %collective-permute-done.114.refs_1_ = bf16[192,1152]{1,0:T(8,128)(2,1)S(1)} collective-permute-done((bf16[192,1152]{1,0:T(8,128)(2,1)}, bf16[192,1152]{1,0:T(8,128)(2,1)S(1)}, u32[]{:S(2)}, u32[]{:S(2)}) %collective-permute-start.114) | collective-permute-done | bytes 442400 | tf_op jit(solution)/shard_map/ppermute | solution.py:192
  115.5 1.4 collective-permute-start.117
  116.8 0.6 collective-permute-start.118
  117.5 0.0 collective-permute-done.115.refs_4_.refs_3_.refs_2_
  117.5 0.0 collective-permute-start.116
  117.5 9.0 %collective-permute-done.117.refs_0_ = bf16[192,1152]{1,0:T(8,128)(2,1)} collective-permute-done((bf16[192,1152]{1,0:T(8,128)(2,1)}, bf16[192,1152]{1,0:T(8,128)(2,1)}, u32[]{:S(2)}, u32[]{:S(2)}) %collective-permute-start.117) | collective-permute-done | bytes 442400 | tf_op jit(solution)/shard_map/ppermute | solution.py:191
  126.5 1.1 collective-permute-start.119
  127.6 0.0 collective-permute-done.118.refs_1_
  127.6 0.9 collective-permute-start.120
  128.5 8.2 %collective-permute-done.119.refs_0_ = bf16[192,1152]{1,0:T(8,128)(2,1)} collective-permute-done((bf16[192,1152]{1,0:T(8,128)(2,1)}, bf16[192,1152]{1,0:T(8,128)(2,1)}, u32[]{:S(2)}, u32[]{:S(2)}) %collective-permute-start.119) | collective-permute-done | bytes 442400 | tf_op jit(solution)/shard_map/ppermute | solution.py:191
  136.7 0.6 collective-permute-done.120.refs_1_
  137.3 1.8 broadcast_select_fusion.3
  139.1 1.5 collective-permute-start.121
  140.6 7.2 %collective-permute-done.121.refs_0_ = bf16[192,1152]{1,0:T(8,128)(2,1)} collective-permute-done((bf16[192,1152]{1,0:T(8,128)(2,1)}, bf16[192,1152]{1,0:T(8,128)(2,1)}, u32[]{:S(2)}, u32[]{:S(2)}) %collective-permute-start.121) | collective-permute-done | bytes 442400 | tf_op jit(solution)/shard_map/ppermute | solution.py:217
  147.7 0.0 collective-permute-done.116.refs_6_.refs_5_.refs_4_
  147.8 1.1 copy-done.2
  148.9 5.1 %shard_map.115 = bf16[192,1024]{1,0:T(8,128)(2,1)} custom-call(s32[1]{0:T(128)} %bitcast.4.slot_ref, bf16[192,1152]{1,0:T(8,128)(2,1)} %collective-permute-done.121.refs_0_, bf16[1,3,1024,256]{3,2,1,0:T(8,128)(2,1)S(1)} %copy-done, bf16[1,3,1024,256]{3,2,1,0:T(8,128)(2,1)} %collective-permute-done.115.refs_4_.refs_3_.refs_2_, ...), custom_call_target="tpu_custom_call" | custom-call | flops 1207959552 | bytes 7471104 | tf_op jit(solution)/shard_map/pallas_call | solution.py:135
  154.0 1.5 collective-permute-start.122
  155.5 6.5 %shard_map.114 = (f32[192,1024]{1,0:T(8,128)}, f32[192,1024]{1,0:T(8,128)}) custom-call(s32[1]{0:T(128)} %bitcast.4.slot_ref, bf16[192,1152]{1,0:T(8,128)(2,1)} %collective-permute-done.119.refs_0_, bf16[192,1152]{1,0:T(8,128)(2,1)} %collective-permute-done.120.refs_1_, bf16[1,3,1024,256]{3,2,1,0:T(8,128)(2,1)S(1)} %copy-done, ...), custom_call_target="tpu_custom_call" | custom-call | flops 2415919104 | bytes 8650752 | tf_op jit(solution)/shard_map/pallas_call | solution.py:135
  162.0 0.0 collective-permute-done.122
  162.0 1.6 fusion.1
  163.6 1.2 collective-permute-start.123
  164.8 0.6 fusion.4
  166.1 0.9 collective-permute-start.126
  167.0 6.5 %shard_map.113 = (f32[192,1024]{1,0:T(8,128)}, f32[192,1024]{1,0:T(8,128)}) custom-call(s32[1]{0:T(128)} %bitcast.4.slot_ref, bf16[192,1152]{1,0:T(8,128)(2,1)} %collective-permute-done.117.refs_0_, bf16[192,1152]{1,0:T(8,128)(2,1)} %collective-permute-done.118.refs_1_, bf16[1,3,1024,256]{3,2,1,0:T(8,128)(2,1)S(1)} %copy-done, ...), custom_call_target="tpu_custom_call" | custom-call | flops 2415919104 | bytes 8650752 | tf_op jit(solution)/shard_map/pallas_call | solution.py:135
  173.6 1.3 add_convert_fusion.4
  174.9 1.2 collective-permute-start.124
  176.1 0.1 add_convert_fusion.2
  176.2 0.9 collective-permute-start.127
  177.1 7.9 %shard_map.112 = (f32[192,1024]{1,0:T(8,128)}, f32[192,1024]{1,0:T(8,128)}, f32[192,1024]{1,0:T(8,128)}) custom-call(s32[1]{0:T(128)} %bitcast.4.slot_ref, bf16[192,1152]{1,0:T(8,128)(2,1)} %collective-permute-done.113.refs_0_, bf16[192,1152]{1,0:T(8,128)(2,1)} %copy-done.7, bf16[192,1152]{1,0:T(8,128)(2,1)} %concatenate.3.refs_2_, ...), custom_call_target="tpu_custom_call" | custom-call | flops 3623878656 | bytes 9830400 | tf_op jit(solution)/shard_map/pallas_call | solution.py:135
  185.1 1.4 add_convert_fusion.3
  186.4 1.2 collective-permute-start.125
  187.6 0.0 collective-permute-done.127
  187.6 1.2 add_convert_fusion.1
  188.9 0.9 collective-permute-start.128
  189.8 7.5 %convert_select_fusion = (f32[1,3,1024,256]{3,2,1,0:T(8,128)}, f32[1,3,1024,256]{3,2,1,0:T(8,128)}) fusion(f32[1,3,1024,256]{3,2,1,0:T(8,128)} %second_ref.1, bf16[2,3,1024,256]{3,2,1,0:T(8,128)(2,1)} %get-tuple-element.216, bf16[2,3,1024,256]{3,2,1,0:T(8,128)(2,1)} %get-tuple-element.215, pred[]{:T(512)S(6)} %eq.63, pred[]{:T(512)S(6)} %ne.7, ...), kind=kLoop, calls=%fused_computation.7 | loop fusion | flops 4718592 | bytes 18874370 | tf_op jit(solution)/shard_map/jit(_where)/select_n | solution.py:236
  197.3 1.3 broadcast_select_fusion.2
  198.6 0.0 collective-permute-done.128
  198.7 0.9 add_convert_fusion
  (18 shorter events, 0.1 us)
Async XLA Ops:
  0.6 116.9 %collective-permute-start.115 = (bf16[1,3,1024,256]{3,2,1,0:T(8,128)(2,1)}, bf16[1,3,1024,256]{3,2,1,0:T(8,128)(2,1)}, u32[]{:S(2)}, u32[]{:S(2)}) collective-permute-start(bf16[1,3,1024,256]{3,2,1,0:T(8,128)(2,1)} %refs_1_.1), channel_id=1, source_target_pairs={{0,8},{8,0},{16,24},{24,16},{1,9},{9,1},{17,25},{25,17},{2,10},{10... | collective-permute-start | bytes 4718600 | tf_op jit(solution)/shard_map/ppermute | solution.py:195
  4.8 100.0 %collective-permute-start.113 = (bf16[192,1152]{1,0:T(8,128)(2,1)}, bf16[192,1152]{1,0:T(8,128)(2,1)}, u32[]{:S(2)}, u32[]{:S(2)}) collective-permute-start(bf16[192,1152]{1,0:T(8,128)(2,1)} %concatenate.3.refs_2_), channel_id=1, source_target_pairs={{0,2},{2,4},{4,6},{6,7},{7,5},{5,3},{3,1},{1,0},{8,10},{10,12},{12... | collective-permute-start | bytes 1327112 | tf_op jit(solution)/shard_map/ppermute | solution.py:191
  10.1 5.3 %copy-start.5 = (s32[8]{0:T(128)S(1)}, s32[8]{0:T(128)}, u32[]{:S(2)}) copy-start(s32[8]{0:T(128)} %param.40) | copy-start | bytes 100
  10.1 5.3 %copy-start.6 = (s32[8]{0:T(128)S(1)}, s32[8]{0:T(128)}, u32[]{:S(2)}) copy-start(s32[8]{0:T(128)} %param.41) | copy-start | bytes 100
  10.1 6.7 %copy-start = (bf16[1,3,1024,256]{3,2,1,0:T(8,128)(2,1)S(1)}, bf16[1,3,1024,256]{3,2,1,0:T(8,128)(2,1)}, u32[]{:S(2)}) copy-start(bf16[1,3,1024,256]{3,2,1,0:T(8,128)(2,1)} %refs_1_.1) | copy-start | bytes 4718596
  16.9 7.0 %collective-permute-start.17 = (bf16[2,3,1024,256]{3,2,1,0:T(8,128)(2,1)}, bf16[2,3,1024,256]{3,2,1,0:T(8,128)(2,1)}, u32[]{:S(2)}, u32[]{:S(2)}) collective-permute-start(bf16[2,3,1024,256]{3,2,1,0:T(8,128)(2,1)} %get-tuple-element.127), channel_id=1, source_target_pairs={{1,3},{3,1},{17,19},{19,17},{9,8},{11,10},{25,24},{27,26}} | collective-permute-start | bytes 9437192 | tf_op jit(solution)/shard_map/cond/branch_4_fun/ppermute | solution.py:42
  23.8 79.8 %collective-permute-start.18 = (bf16[2,3,1024,256]{3,2,1,0:T(8,128)(2,1)}, bf16[2,3,1024,256]{3,2,1,0:T(8,128)(2,1)}, u32[]{:S(2)}, u32[]{:S(2)}) collective-permute-start(bf16[2,3,1024,256]{3,2,1,0:T(8,128)(2,1)} %collective-permute-done.17), channel_id=1, source_target_pairs={{8,11},{10,9},{24,27},{26,25}} | collective-permute-start | bytes 9437192 | tf_op jit(solution)/shard_map/cond/branch_4_fun/ppermute | solution.py:44
  26.2 42.6 %collective-permute-start.16 = (bf16[1,3,1024,256]{3,2,1,0:T(8,128)(2,1)S(1)}, bf16[1,3,1024,256]{3,2,1,0:T(8,128)(2,1)}, u32[]{:S(2)}, u32[]{:S(2)}) collective-permute-start(bf16[1,3,1024,256]{3,2,1,0:T(8,128)(2,1)S(1)} %get-tuple-element.126), channel_id=1, source_target_pairs={{1,3},{3,1},{17,19},{19,17},{9,11},{11,9},{25,27},{27,25}} | collective-permute-start | bytes 4718600 | tf_op jit(solution)/shard_map/cond/branch_4_fun/ppermute | solution.py:43
  66.9 36.8 %collective-permute-start.19 = (bf16[1,3,1024,256]{3,2,1,0:T(8,128)(2,1)S(1)}, bf16[1,3,1024,256]{3,2,1,0:T(8,128)(2,1)}, u32[]{:S(2)}, u32[]{:S(2)}) collective-permute-start(bf16[1,3,1024,256]{3,2,1,0:T(8,128)(2,1)S(1)} %get-tuple-element.126), channel_id=1, source_target_pairs={{0,16},{8,24},{16,0},{24,8},{1,17},{9,25},{17,1},{25,9},{2,18},{10... | collective-permute-start | bytes 4718600 | tf_op jit(solution)/shard_map/cond/branch_4_fun/ppermute | solution.py:164
  103.7 11.8 %collective-permute-start.114 = (bf16[192,1152]{1,0:T(8,128)(2,1)}, bf16[192,1152]{1,0:T(8,128)(2,1)S(1)}, u32[]{:S(2)}, u32[]{:S(2)}) collective-permute-start(bf16[192,1152]{1,0:T(8,128)(2,1)} %concatenate.3.refs_2_), channel_id=1, source_target_pairs={{2,0},{4,2},{6,4},{7,6},{5,7},{3,5},{1,3},{0,1},{10,8},{12,10},{14... | collective-permute-start | bytes 1327112 | tf_op jit(solution)/shard_map/ppermute | solution.py:192
  115.5 2.0 %copy-start.7 = (bf16[192,1152]{1,0:T(8,128)(2,1)}, bf16[192,1152]{1,0:T(8,128)(2,1)S(1)}, u32[]{:S(2)}) copy-start(bf16[192,1152]{1,0:T(8,128)(2,1)S(1)} %collective-permute-done.114.refs_1_) | copy-start | bytes 1327108
  115.5 11.1 %collective-permute-start.117 = (bf16[192,1152]{1,0:T(8,128)(2,1)}, bf16[192,1152]{1,0:T(8,128)(2,1)}, u32[]{:S(2)}, u32[]{:S(2)}) collective-permute-start(bf16[192,1152]{1,0:T(8,128)(2,1)} %collective-permute-done.113.refs_0_), channel_id=1, source_target_pairs={{0,2},{2,4},{4,6},{6,7},{7,5},{5,3},{3,1},{1,0},{8,10},{10,12},{12... | collective-permute-start | bytes 1327112 | tf_op jit(solution)/shard_map/ppermute | solution.py:191
  116.8 10.8 %collective-permute-start.118 = (bf16[192,1152]{1,0:T(8,128)(2,1)S(1)}, bf16[192,1152]{1,0:T(8,128)(2,1)}, u32[]{:S(2)}, u32[]{:S(2)}) collective-permute-start(bf16[192,1152]{1,0:T(8,128)(2,1)S(1)} %collective-permute-done.114.refs_1_), channel_id=1, source_target_pairs={{2,0},{4,2},{6,4},{7,6},{5,7},{3,5},{1,3},{0,1},{10,8},{12,10},{14... | collective-permute-start | bytes 1327112 | tf_op jit(solution)/shard_map/ppermute | solution.py:192
  117.5 30.3 %collective-permute-start.116 = (bf16[1,3,1024,256]{3,2,1,0:T(8,128)(2,1)}, bf16[1,3,1024,256]{3,2,1,0:T(8,128)(2,1)S(1)}, u32[]{:S(2)}, u32[]{:S(2)}) collective-permute-start(bf16[1,3,1024,256]{3,2,1,0:T(8,128)(2,1)} %get-tuple-element.206.refs_5_.refs_4_.refs_3_), channel_id=1, source_target_pairs={{0,8},{8,0},{16,24},{24,16},{1,9},{9,1},{17,25},{25,17},{2,10},{10... | collective-permute-start | bytes 4718600 | tf_op jit(solution)/shard_map/ppermute | solution.py:205
  126.5 10.2 %collective-permute-start.119 = (bf16[192,1152]{1,0:T(8,128)(2,1)}, bf16[192,1152]{1,0:T(8,128)(2,1)}, u32[]{:S(2)}, u32[]{:S(2)}) collective-permute-start(bf16[192,1152]{1,0:T(8,128)(2,1)} %collective-permute-done.117.refs_0_), channel_id=1, source_target_pairs={{0,2},{2,4},{4,6},{6,7},{7,5},{5,3},{3,1},{1,0},{8,10},{10,12},{12... | collective-permute-start | bytes 1327112 | tf_op jit(solution)/shard_map/ppermute | solution.py:191
  127.6 9.7 %collective-permute-start.120 = (bf16[192,1152]{1,0:T(8,128)(2,1)}, bf16[192,1152]{1,0:T(8,128)(2,1)}, u32[]{:S(2)}, u32[]{:S(2)}) collective-permute-start(bf16[192,1152]{1,0:T(8,128)(2,1)} %collective-permute-done.118.refs_1_), channel_id=1, source_target_pairs={{2,0},{4,2},{6,4},{7,6},{5,7},{3,5},{1,3},{0,1},{10,8},{12,10},{14... | collective-permute-start | bytes 1327112 | tf_op jit(solution)/shard_map/ppermute | solution.py:192
  139.1 8.6 %collective-permute-start.121 = (bf16[192,1152]{1,0:T(8,128)(2,1)}, bf16[192,1152]{1,0:T(8,128)(2,1)}, u32[]{:S(2)}, u32[]{:S(2)}) collective-permute-start(bf16[192,1152]{1,0:T(8,128)(2,1)} %broadcast_select_fusion.3), channel_id=1, source_target_pairs={{0,2},{2,4},{4,6},{6,7},{7,5},{5,3},{3,1},{1,0},{10,8},{12,10},{14... | collective-permute-start | bytes 1327112 | tf_op jit(solution)/shard_map/ppermute | solution.py:217
  147.7 1.1 copy-start.2
  154.0 8.0 %collective-permute-start.122 = (bf16[192,1024]{1,0:T(8,128)(2,1)}, bf16[192,1024]{1,0:T(8,128)(2,1)S(1)}, u32[]{:S(2)}, u32[]{:S(2)}) collective-permute-start(bf16[192,1024]{1,0:T(8,128)(2,1)} %shard_map.115), channel_id=1, source_target_pairs={{0,2},{2,4},{4,6},{6,7},{7,5},{5,3},{3,1},{1,0},{10,8},{12,10},{14... | collective-permute-start | bytes 1179656 | tf_op jit(solution)/shard_map/ppermute | solution.py:222
  163.6 10.0 %collective-permute-start.123 = (bf16[192,1024]{1,0:T(8,128)(2,1)S(1)}, bf16[192,1024]{1,0:T(8,128)(2,1)S(1)}, u32[]{:S(2)}, u32[]{:S(2)}) collective-permute-start(bf16[192,1024]{1,0:T(8,128)(2,1)S(1)} %get-tuple-element.224), channel_id=1, source_target_pairs={{2,0},{4,2},{6,4},{7,6},{5,7},{3,5},{1,3},{0,1},{10,8},{12,10},{14... | collective-permute-start | bytes 1179656 | tf_op jit(solution)/shard_map/ppermute | solution.py:228
  166.1 10.0 %collective-permute-start.126 = (bf16[192,1024]{1,0:T(8,128)(2,1)S(1)}, bf16[192,1024]{1,0:T(8,128)(2,1)S(1)}, u32[]{:S(2)}, u32[]{:S(2)}) collective-permute-start(bf16[192,1024]{1,0:T(8,128)(2,1)S(1)} %get-tuple-element.225), channel_id=1, source_target_pairs={{0,2},{2,4},{4,6},{6,7},{7,5},{5,3},{3,1},{1,0},{8,10},{10,12},{12... | collective-permute-start | bytes 1179656 | tf_op jit(solution)/shard_map/ppermute | solution.py:229
  173.6 2.5 %copy-start.3 = (f32[192,1024]{1,0:T(8,128)S(1)}, f32[192,1024]{1,0:T(8,128)}, u32[]{:S(2)}) copy-start(f32[192,1024]{1,0:T(8,128)} %get-tuple-element.212) | copy-start | bytes 2359300
  174.9 10.2 %collective-permute-start.124 = (bf16[192,1024]{1,0:T(8,128)(2,1)S(1)}, bf16[192,1024]{1,0:T(8,128)(2,1)S(1)}, u32[]{:S(2)}, u32[]{:S(2)}) collective-permute-start(bf16[192,1024]{1,0:T(8,128)(2,1)S(1)} %add_convert_fusion.4), channel_id=1, source_target_pairs={{2,0},{4,2},{6,4},{7,6},{5,7},{3,5},{1,3},{0,1},{10,8},{12,10},{14... | collective-permute-start | bytes 1179656 | tf_op jit(solution)/shard_map/ppermute | solution.py:228
  176.2 11.5 %collective-permute-start.127 = (bf16[192,1024]{1,0:T(8,128)(2,1)S(1)}, bf16[192,1024]{1,0:T(8,128)(2,1)S(1)}, u32[]{:S(2)}, u32[]{:S(2)}) collective-permute-start(bf16[192,1024]{1,0:T(8,128)(2,1)S(1)} %add_convert_fusion.2), channel_id=1, source_target_pairs={{0,2},{2,4},{4,6},{6,7},{7,5},{5,3},{3,1},{1,0},{8,10},{10,12},{12... | collective-permute-start | bytes 1179656 | tf_op jit(solution)/shard_map/ppermute | solution.py:229
  185.1 4.7 %copy-start.1 = (f32[1,3,1024,256]{3,2,1,0:T(8,128)S(1)}, f32[1,3,1024,256]{3,2,1,0:T(8,128)}, u32[]{:S(2)}) copy-start(f32[1,3,1024,256]{3,2,1,0:T(8,128)} %first_ref.1) | copy-start | bytes 9437188
  186.4 12.2 %collective-permute-start.125 = (bf16[192,1024]{1,0:T(8,128)(2,1)S(1)}, bf16[192,1024]{1,0:T(8,128)(2,1)S(1)}, u32[]{:S(2)}, u32[]{:S(2)}) collective-permute-start(bf16[192,1024]{1,0:T(8,128)(2,1)S(1)} %add_convert_fusion.3), channel_id=1, source_target_pairs={{2,0},{4,2},{6,4},{7,6},{5,7},{3,5},{1,3},{0,1},{10,8},{12,10},{14... | collective-permute-start | bytes 1179656 | tf_op jit(solution)/shard_map/ppermute | solution.py:228
  188.9 9.8 %collective-permute-start.128 = (bf16[192,1024]{1,0:T(8,128)(2,1)S(1)}, bf16[192,1024]{1,0:T(8,128)(2,1)S(1)}, u32[]{:S(2)}, u32[]{:S(2)}) collective-permute-start(bf16[192,1024]{1,0:T(8,128)(2,1)S(1)} %add_convert_fusion.1), channel_id=1, source_target_pairs={{0,2},{2,4},{4,6},{6,7},{7,5},{5,3},{3,1},{1,0},{8,10},{10,12},{12... | collective-permute-start | bytes 1179656 | tf_op jit(solution)/shard_map/ppermute | solution.py:229
  197.3 1.3 copy-start.4
